TPU v7x, 32 devices: a whole 2x2x4 slice. The times are simulated.
32 devices in a mesh: dp: 8 (over z, core), seq: 4 (over y, x).
Axes of the slice: x: 2, y: 2, z: 4, core: 2. Of those that a mesh axis runs over, the one named last changes fastest.
Arguments:
- hidden_in: bfloat16 [8, 2048, 1088], P('dp', 'seq'), may hold values from -6 to 6
- segments: int32 [8, 2048], P('dp'), may hold values from 0 to 3, never falling along the last dimension, each value on 1 to 1024 neighbouring positions
- cotangent: bfloat16 [8, 2048, 1088], P('dp', 'seq'), may hold values from -6 to 6
- w_qkv: bfloat16 [27904, 128], P(('dp', 'seq')), may hold values from -0.1875 to 0.1875
- w_out: bfloat16 [9472, 128], P(('dp', 'seq')), may hold values from -1 to 1
- w_up: bfloat16 [37120, 128], P(('dp', 'seq')), may hold values from -0.1875 to 0.1875
- w_down: bfloat16 [37120, 128], P(('dp', 'seq')), may hold values from -0.09375 to 0.09375
- vectors: bfloat16 [256, 128], P(('dp', 'seq')), may hold values from -1.21 to 1.3
Outputs:
- hidden_out: bfloat16 [8, 2048, 1088], P('dp', 'seq')
- grad_in: float32 [8, 2048, 1088], P('dp', 'seq')
- grad_qkv: float32 [27904, 128], P(('dp', 'seq'))
- grad_out_proj: float32 [9472, 128], P(('dp', 'seq'))
- grad_up: float32 [37120, 128], P(('dp', 'seq'))
- grad_down: float32 [37120, 128], P(('dp', 'seq'))
- grad_vectors: float32 [256, 128], P(('dp', 'seq'))
Inputs may be any that keep to these rules, and one draw needn't show every extreme that they name: `segments`: in each sequence the segment numbers never fall; a segment covers 1 to 1024 positions and one covers exactly that many.
All inputs are finite; a program needn't handle non-finite values.
Results may differ from a plain program's by a relative error of at most 0.019.
Values may be sent and summed in bfloat16 or wider, within the bound.
A program may use at most 256 MiB of HBM per device.

v0:
```python
import math

import jax
import jax.numpy as jnp
from jax import lax
from jax.sharding import PartitionSpec as P

HEADS = 17
FF = 4352


eps_norm = 1e-05
masked_score = -1e30


def layer_norm(values, gain_vec, shift_vec):
    centre = jnp.mean(values, axis=-1, keepdims=True)
    centred = values - centre
    spread = jnp.mean(centred * centred, axis=-1, keepdims=True)
    return centred * lax.rsqrt(spread + eps_norm) * gain_vec + shift_vec


def unpack(flat_values, model_width, hidden_units):
    gain_one = flat_values[0:model_width]
    shift_one = flat_values[model_width : 2 * model_width]
    bias_query = flat_values[2 * model_width : 3 * model_width]
    bias_value = flat_values[3 * model_width : 4 * model_width]
    bias_proj = flat_values[4 * model_width : 5 * model_width]
    gain_two = flat_values[5 * model_width : 6 * model_width]
    shift_two = flat_values[6 * model_width : 7 * model_width]
    bias_up = flat_values[7 * model_width : 7 * model_width + hidden_units]
    bias_down = flat_values[7 * model_width + hidden_units : 8 * model_width + hidden_units]
    return (
        gain_one,
        shift_one,
        bias_query,
        bias_value,
        bias_proj,
        gain_two,
        shift_two,
        bias_up,
        bias_down,
    )


def take_matrix(flat_rows, row_count, col_count):
    return flat_rows.reshape(-1)[: row_count * col_count].reshape(row_count, col_count)


def to_flat(grad_matrix, row_count):
    flat_values = grad_matrix.reshape(-1)
    return jnp.pad(flat_values, (0, row_count * 128 - flat_values.shape[0])).reshape(row_count, 128)


def shape_weights(gathered, model_width):
    return (
        take_matrix(gathered[0], model_width, 3 * model_width),
        take_matrix(gathered[1], model_width, model_width),
        take_matrix(gathered[2], model_width, FF),
        take_matrix(gathered[3], FF, model_width),
        gathered[4],
    )


def fetch_forward(w_qkv, w_out, w_up, w_down, vectors):
    by_column = (
        lax.all_gather(w_qkv, "seq", axis=0, tiled=True),
        lax.all_gather(w_out, "seq", axis=0, tiled=True),
        lax.all_gather(w_up, "seq", axis=0, tiled=True),
        lax.all_gather(w_down, "seq", axis=0, tiled=True),
        lax.all_gather(vectors, "seq", axis=0, tiled=True),
    )
    return (
        lax.all_gather(by_column[0], "dp", axis=0, tiled=True),
        lax.all_gather(by_column[1], "dp", axis=0, tiled=True),
        lax.all_gather(by_column[2], "dp", axis=0, tiled=True),
        lax.all_gather(by_column[3], "dp", axis=0, tiled=True),
        lax.all_gather(by_column[4], "dp", axis=0, tiled=True),
    )


def fetch_backward(w_qkv, w_out, w_up, w_down, vectors):
    by_column = (
        lax.all_gather(w_qkv, "seq", axis=0, tiled=True),
        lax.all_gather(w_out, "seq", axis=0, tiled=True),
        lax.all_gather(w_up, "seq", axis=0, tiled=True),
        lax.all_gather(w_down, "seq", axis=0, tiled=True),
        lax.all_gather(vectors, "seq", axis=0, tiled=True),
    )
    return (
        lax.all_gather(by_column[0], "dp", axis=0, tiled=True),
        lax.all_gather(by_column[1], "dp", axis=0, tiled=True),
        lax.all_gather(by_column[2], "dp", axis=0, tiled=True),
        lax.all_gather(by_column[3], "dp", axis=0, tiled=True),
        lax.all_gather(by_column[4], "dp", axis=0, tiled=True),
    )


def reduce_mlp(grad_up_flat, grad_down_flat):
    by_row = (
        lax.psum_scatter(
            grad_up_flat.astype(jnp.bfloat16), "dp", scatter_dimension=0, tiled=True
        ).astype(jnp.float32),
        lax.psum_scatter(
            grad_down_flat.astype(jnp.bfloat16), "dp", scatter_dimension=0, tiled=True
        ).astype(jnp.float32),
    )
    return (
        lax.psum_scatter(
            by_row[0].astype(jnp.bfloat16), "seq", scatter_dimension=0, tiled=True
        ).astype(jnp.float32),
        lax.psum_scatter(
            by_row[1].astype(jnp.bfloat16), "seq", scatter_dimension=0, tiled=True
        ).astype(jnp.float32),
    )


def reduce_attention(grad_qkv_flat, grad_out_flat, grad_vec_flat):
    by_row = (
        lax.psum_scatter(
            grad_qkv_flat.astype(jnp.bfloat16), "dp", scatter_dimension=0, tiled=True
        ).astype(jnp.float32),
        lax.psum_scatter(
            grad_out_flat.astype(jnp.bfloat16), "dp", scatter_dimension=0, tiled=True
        ).astype(jnp.float32),
        lax.psum_scatter(
            grad_vec_flat.astype(jnp.bfloat16), "dp", scatter_dimension=0, tiled=True
        ).astype(jnp.float32),
    )
    return (
        lax.psum_scatter(
            by_row[0].astype(jnp.bfloat16), "seq", scatter_dimension=0, tiled=True
        ).astype(jnp.float32),
        lax.psum_scatter(
            by_row[1].astype(jnp.bfloat16), "seq", scatter_dimension=0, tiled=True
        ).astype(jnp.float32),
        lax.psum_scatter(
            by_row[2].astype(jnp.bfloat16), "seq", scatter_dimension=0, tiled=True
        ).astype(jnp.float32),
    )


def body(hidden_in, segments, cotangent, w_qkv, w_out, w_up, w_down, vectors):
    tok_rows = hidden_in.shape[1]
    model_width = hidden_in.shape[2]
    head_count = HEADS
    head_dim = model_width // head_count
    score_scale = head_dim ** (-0.5)
    length = segments.shape[1]
    block_rows = min(512, length)
    spread_count = lax.axis_size("dp") * lax.axis_size("seq")
    seg_row = segments[0]
    query_first = lax.axis_index("seq") * tok_rows
    query_places = query_first + jnp.arange(tok_rows, dtype=jnp.int32)
    query_segs = lax.dynamic_slice_in_dim(seg_row, query_first, tok_rows)
    fwd_gathered = fetch_forward(w_qkv, w_out, w_up, w_down, vectors)
    fwd_weights = shape_weights(fwd_gathered, model_width)
    hidden_units = FF
    (
        gain_one,
        shift_one,
        bias_query,
        bias_value,
        bias_proj,
        gain_two,
        shift_two,
        bias_up,
        bias_down,
    ) = unpack(fwd_weights[4].reshape(-1).astype(jnp.float32), model_width, hidden_units)
    tokens = hidden_in[0].astype(jnp.float32)
    normed_f, pull_one = jax.vjp(layer_norm, tokens, gain_one, shift_one)
    normed = normed_f.astype(jnp.bfloat16)
    packed = jnp.dot(normed, fwd_weights[0], preferred_element_type=jnp.float32)
    queries = (packed[:, :model_width] + bias_query).astype(jnp.bfloat16)
    key_rows = packed[:, model_width : 2 * model_width].astype(jnp.bfloat16)
    value_rows = (packed[:, 2 * model_width :] + bias_value).astype(jnp.bfloat16)
    query_heads = queries.reshape(tok_rows, head_count, head_dim)

    def visible_scores(key_heads, offset):
        piece_rows = key_heads.shape[0]
        key_places = offset + jnp.arange(piece_rows, dtype=jnp.int32)
        key_segs = lax.dynamic_slice_in_dim(seg_row, offset, piece_rows)
        visible = (query_places[:, None] >= key_places[None, :]) & (
            query_segs[:, None] == key_segs[None, :]
        )
        scores = (
            jnp.einsum("qhd,khd->hqk", query_heads, key_heads, preferred_element_type=jnp.float32)
            * score_scale
        )
        return (jnp.where(visible[None], scores, masked_score), visible)

    def absorb(state_in, key_block, value_block, offset):
        running_max, running_sum, running_out = state_in
        piece_rows = key_block.shape[0]
        key_heads = key_block.reshape(piece_rows, head_count, head_dim)
        value_heads = value_block.reshape(piece_rows, head_count, head_dim)
        scores, visible = visible_scores(key_heads, offset)
        new_max = jnp.maximum(running_max, jnp.max(scores, axis=-1))
        weights = jnp.where(visible[None], jnp.exp(scores - new_max[:, :, None]), 0.0)
        factor = jnp.exp(running_max - new_max)
        running_sum = running_sum * factor + jnp.sum(weights, axis=-1)
        running_out = running_out * factor.T[:, :, None] + jnp.einsum(
            "hqk,khd->qhd",
            weights.astype(jnp.bfloat16),
            value_heads,
            preferred_element_type=jnp.float32,
        )
        return (new_max, running_sum, running_out)

    initial = (
        jnp.full((head_count, tok_rows), masked_score, jnp.float32),
        jnp.zeros((head_count, tok_rows), jnp.float32),
        jnp.zeros((tok_rows, head_count, head_dim), jnp.float32),
    )
    key_all = lax.all_gather(key_rows, "seq", axis=0, tiled=True)
    value_all = lax.all_gather(value_rows, "seq", axis=0, tiled=True)
    piece_rows = key_all.shape[0]
    step_rows = math.gcd(piece_rows, block_rows)

    def advance(state_now, block_index):
        local_first = block_index * step_rows
        key_block = lax.dynamic_slice_in_dim(key_all, local_first, step_rows)
        value_block = lax.dynamic_slice_in_dim(value_all, local_first, step_rows)
        return (absorb(state_now, key_block, value_block, local_first), None)

    state_out, _ = lax.scan(advance, initial, jnp.arange(piece_rows // step_rows, dtype=jnp.int32))
    running_max, running_sum, running_out = state_out
    attended_f = running_out / running_sum.T[:, :, None]
    log_total = running_max + jnp.log(running_sum)
    attended = attended_f.reshape(tok_rows, model_width).astype(jnp.bfloat16)
    middle = (
        tokens + jnp.dot(attended, fwd_weights[1], preferred_element_type=jnp.float32) + bias_proj
    )
    normed_two_f, pull_two = jax.vjp(layer_norm, middle, gain_two, shift_two)
    normed_two = normed_two_f.astype(jnp.bfloat16)
    before = jnp.dot(normed_two, fwd_weights[2], preferred_element_type=jnp.float32) + bias_up
    active_f, pull_gelu = jax.vjp(jax.nn.gelu, before)
    active = active_f.astype(jnp.bfloat16)
    result = (
        middle + jnp.dot(active, fwd_weights[3], preferred_element_type=jnp.float32) + bias_down
    )
    hidden_out = result.astype(jnp.bfloat16)[None]
    back_weights = shape_weights(fetch_backward(w_qkv, w_out, w_up, w_down, vectors), model_width)
    cot_rows = cotangent[0]
    cot_float = cot_rows.astype(jnp.float32)
    grad_down_full = jnp.dot(active.T, cot_rows, preferred_element_type=jnp.float32)
    d_bias_down = jnp.sum(cot_float, axis=0)
    d_active = jnp.dot(cot_rows, back_weights[3].T, preferred_element_type=jnp.float32)
    d_before = pull_gelu(d_active)[0].astype(jnp.bfloat16)
    d_bias_up = jnp.sum(d_before.astype(jnp.float32), axis=0)
    grad_up_full = jnp.dot(normed_two.T, d_before, preferred_element_type=jnp.float32)
    d_normed_two = jnp.dot(d_before, back_weights[2].T, preferred_element_type=jnp.float32)
    d_middle_norm, d_gain_two, d_shift_two = pull_two(d_normed_two)
    d_middle = cot_float + d_middle_norm
    mlp_grads = reduce_mlp(
        to_flat(grad_up_full, w_up.shape[0] * spread_count),
        to_flat(grad_down_full, w_down.shape[0] * spread_count),
    )
    d_proj = d_middle.astype(jnp.bfloat16)
    d_bias_proj = jnp.sum(d_middle, axis=0)
    grad_out_full = jnp.dot(attended.T, d_proj, preferred_element_type=jnp.float32)
    d_attended = jnp.dot(d_proj, back_weights[1].T, preferred_element_type=jnp.float32).astype(
        jnp.bfloat16
    )
    d_heads = d_attended.reshape(tok_rows, head_count, head_dim)
    row_dots = jnp.einsum("qhd,qhd->hq", d_heads.astype(jnp.float32), attended_f)
    back_keys, back_values = (
        lax.all_gather(key_rows, "seq", axis=0, tiled=True),
        lax.all_gather(value_rows, "seq", axis=0, tiled=True),
    )

    def back_block(block_index):
        offset = block_index * block_rows
        key_heads = lax.dynamic_slice_in_dim(back_keys, offset, block_rows).reshape(
            block_rows, head_count, head_dim
        )
        value_heads = lax.dynamic_slice_in_dim(back_values, offset, block_rows).reshape(
            block_rows, head_count, head_dim
        )
        scores, visible = visible_scores(key_heads, offset)
        probs = jnp.where(visible[None], jnp.exp(scores - log_total[:, :, None]), 0.0)
        d_probs = jnp.einsum(
            "qhd,khd->hqk", d_heads, value_heads, preferred_element_type=jnp.float32
        )
        d_scores = (probs * (d_probs - row_dots[:, :, None])).astype(jnp.bfloat16)
        return (key_heads, probs, d_scores)

    zero_dq = jnp.zeros((tok_rows, head_count, head_dim), jnp.float32)
    block_ids = jnp.arange(length // block_rows, dtype=jnp.int32)

    def back_step(dq_now, block_index):
        key_heads, probs, d_scores = back_block(block_index)
        dq_now = dq_now + score_scale * jnp.einsum(
            "hqk,khd->qhd", d_scores, key_heads, preferred_element_type=jnp.float32
        )
        d_key_block = score_scale * jnp.einsum(
            "hqk,qhd->khd", d_scores, query_heads, preferred_element_type=jnp.float32
        )
        d_value_block = jnp.einsum(
            "hqk,qhd->khd", probs.astype(jnp.bfloat16), d_heads, preferred_element_type=jnp.float32
        )
        return (
            dq_now,
            (
                d_key_block.reshape(block_rows, model_width),
                d_value_block.reshape(block_rows, model_width),
            ),
        )

    dq_sum, (key_parts, value_parts) = lax.scan(back_step, zero_dq, block_ids)
    key_terms = key_parts.reshape(length, model_width)
    value_terms = value_parts.reshape(length, model_width)
    d_key_sum, d_value_sum = (
        lax.psum_scatter(
            key_terms.astype(jnp.bfloat16), "seq", scatter_dimension=0, tiled=True
        ).astype(jnp.float32),
        lax.psum_scatter(
            value_terms.astype(jnp.bfloat16), "seq", scatter_dimension=0, tiled=True
        ).astype(jnp.float32),
    )
    d_query = dq_sum.reshape(tok_rows, model_width).astype(jnp.bfloat16)
    d_key = d_key_sum.astype(jnp.bfloat16)
    d_value = d_value_sum.astype(jnp.bfloat16)
    d_packed = jnp.concatenate([d_query, d_key, d_value], axis=1)
    grad_qkv_full = jnp.dot(normed.T, d_packed, preferred_element_type=jnp.float32)
    d_normed = jnp.dot(d_packed, back_weights[0].T, preferred_element_type=jnp.float32)
    d_tokens_norm, d_gain_one, d_shift_one = pull_one(d_normed)
    grad_in = (d_middle + d_tokens_norm)[None]
    vector_grads = jnp.concatenate(
        [
            d_gain_one,
            d_shift_one,
            jnp.sum(d_query.astype(jnp.float32), axis=0),
            jnp.sum(d_value.astype(jnp.float32), axis=0),
            d_bias_proj,
            d_gain_two,
            d_shift_two,
            d_bias_up,
            d_bias_down,
        ]
    )
    attn_grads = reduce_attention(
        to_flat(grad_qkv_full, w_qkv.shape[0] * spread_count),
        to_flat(grad_out_full, w_out.shape[0] * spread_count),
        to_flat(vector_grads, vectors.shape[0] * spread_count),
    )
    return (
        hidden_out,
        grad_in,
        attn_grads[0],
        attn_grads[1],
        mlp_grads[0],
        mlp_grads[1],
        attn_grads[2],
    )


def solution(mesh):
    return jax.shard_map(
        body,
        mesh=mesh,
        in_specs=(
            P("dp", "seq", None),
            P("dp", None),
            P("dp", "seq", None),
            P(("dp", "seq"), None),
            P(("dp", "seq"), None),
            P(("dp", "seq"), None),
            P(("dp", "seq"), None),
            P(("dp", "seq"), None),
        ),
        out_specs=(
            P("dp", "seq", None),
            P("dp", "seq", None),
            P(("dp", "seq"), None),
            P(("dp", "seq"), None),
            P(("dp", "seq"), None),
            P(("dp", "seq"), None),
            P(("dp", "seq"), None),
        ),
        check_vma=False,
    )
```

profile of v0, /device:TPU:0, one launch (start us, length us, event | category | flops | bytes accessed | tf_op | source)
XLA Modules:
  0.0 1439.9 jit_solution(305809306453072882)
XLA Ops:
  8.7 19.3 %all_gather.48 = bf16[3488,128]{1,0:T(8,128)(2,1)} all-gather(bf16[872,128]{1,0:T(8,128)(2,1)} %param.15), channel_id=1, replica_groups=mesh['dp'=8,'seq'=4] {'seq'}, dimensions={0}, use_global_device_ids=true | all-gather | bytes 1116160 | tf_op jit(solution)/shard_map/all_gather | solution.py:67
  43.2 29.6 %all-gather.21.cloned.1.call-done = bf16[4640,128]{1,0:T(8,128)(2,1)} async-done(((bf16[1160,128]{1,0:T(8,128)(2,1)}), bf16[4640,128]{1,0:T(8,128)(2,1)}) %all-gather.21.cloned.1.call-update) | async-done | bytes 1187856 | tf_op jit(solution)/shard_map/all_gather | solution.py:70
  80.9 14.2 all_gather.47
  96.9 49.7 %all-gather.9.cloned.1.call-done = bf16[27904,128]{1,0:T(8,128)(2,1)} async-done(((bf16[3488,128]{1,0:T(8,128)(2,1)}), bf16[27904,128]{1,0:T(8,128)(2,1)}) %all-gather.9.cloned.1.call-update) | async-done | bytes 7143440 | tf_op jit(solution)/shard_map/all_gather | solution.py:74
  153.1 13.1 reshape.331
  185.2 85.5 %all-gather.19.cloned.1.call-done = bf16[37120,128]{1,0:T(8,128)(2,1)} async-done(((bf16[4640,128]{1,0:T(8,128)(2,1)}), bf16[37120,128]{1,0:T(8,128)(2,1)}) %all-gather.19.cloned.1.call-update) | async-done | bytes 9502736 | tf_op jit(solution)/shard_map/all_gather | solution.py:76
  279.9 18.0 %reshape.334 = bf16[1088,4352]{1,0:T(8,128)(2,1)} reshape(bf16[36992,128]{1,0:T(8,128)(2,1)} %slice.85) | data formatting | bytes 18939904 | tf_op jit(solution)/shard_map/reshape | solution.py:47
  297.9 64.1 %all-gather.23.cloned.1.call-done = bf16[37120,128]{1,0:T(8,128)(2,1)} async-done(((bf16[4640,128]{1,0:T(8,128)(2,1)}), bf16[37120,128]{1,0:T(8,128)(2,1)}) %all-gather.23.cloned.1.call-update) | async-done | bytes 9502736 | tf_op jit(solution)/shard_map/all_gather | solution.py:77
  371.1 17.1 %reshape.335 = bf16[4352,1088]{1,0:T(8,128)(2,1)} reshape(bf16[36992,128]{1,0:T(8,128)(2,1)} %slice.87) | data formatting | bytes 18939904 | tf_op jit(solution)/shard_map/reshape | solution.py:47
  388.3 28.7 %all-gather.13.cloned.1.call-done = bf16[2048,1088]{0,1:T(8,128)(2,1)} async-done(((bf16[512,1088]{0,1:T(8,128)(2,1)}), bf16[2048,1088]{0,1:T(8,128)(2,1)}) %all-gather.13.cloned.1.call-update) | async-done | bytes 4456464 | tf_op jit(solution)/shard_map/all_gather | solution.py:216
  417.0 57.2 %all-gather.11.cloned.1.call-done = bf16[2048,1088]{0,1:T(8,128)(2,1)} async-done(((bf16[512,1088]{0,1:T(8,128)(2,1)}), bf16[2048,1088]{0,1:T(8,128)(2,1)}) %all-gather.11.cloned.1.call-update) | async-done | bytes 4456464 | tf_op jit(solution)/shard_map/all_gather | solution.py:215
  474.2 128.4 %while.30 = (s32[]{:T(128)}, f32[17,512]{1,0:T(8,128)S(1)}, f32[17,512]{1,0:T(8,128)S(1)}, f32[512,17,64]{0,2,1:T(8,128)}, s32[4]{0:T(128)S(1)}, /*index=5*/s32[...) while((s32[]{:T(128)}, f32[17,512]{1,0:T(8,128)S(1)}, ...), condition=%wide.region_5.6_spmd.clone, body=%wide.region_2.5_spmd.clone.sunk | while | flops 1201295360 | bytes 67354856 | solution.py:226
  609.7 12.5 fusion.84
  622.2 16.1 %fusion.90 = (bf16[4352]{0:T(1024)(128)(2,1)}, bf16[512,4352]{1,0:T(8,128)(2,1)}) fusion(f32[512,4352]{1,0:T(8,128)} %fusion.84, f32[4352]{0:T(1024)S(1)} %copy-done.38, bf16[4352,1088]{1,0:T(8,128)(2,1)} %reshape.335, bf16[1,512,1088]{1,2,0:T(8,128)(2,1)S(1)} %copy-done.11), kind=kOutput, calls=%fused_computation.147 | convolution fusion | flops 4897632256 | bytes 23979520 | tf_op jit(solution)/shard_map/dot_general | solution.py:248
  654.6 173.6 %while.31 = (s32[]{:T(128)}, f32[512,17,64]{0,2,1:T(8,128)S(1)}, bf16[4,512,1088]{1,2,0:T(8,128)(2,1)}, bf16[4,512,1088]{1,2,0:T(8,128)(2,1)}, s32[4]{0:T(128)S(...) while((s32[]{:T(128)}, f32[512,17,64]{0,2,1:T(8,128)S(1)}, ...), condition=%wide.region_11.12_spmd.clone, body=%wide.region_10.11_spmd.clone.sunk | while | flops 2909176832 | bytes 117889384 | solution.py:310
  669.5 12.0 fusion.159
  712.8 12.0 fusion.159
  756.1 12.0 fusion.159
  799.4 12.0 fusion.159
  870.8 12.8 convolution_convert_fusion
  883.6 13.9 copy.44
  897.5 19.5 %reshape.340 = bf16[4734976]{0:T(1024)(128)(2,1)} reshape(bf16[4352,1088]{1,0:T(8,128)(2,1)} %copy.44) | data formatting | bytes 18939904 | tf_op jit(solution)/shard_map/reshape | solution.py:51
  937.8 18.5 %reshape.339 = bf16[4734976]{0:T(1024)(128)(2,1)} reshape(bf16[1088,4352]{1,0:T(8,128)(2,1)} %convolution_convert_fusion.1) | data formatting | bytes 18939904 | tf_op jit(solution)/shard_map/reshape | solution.py:51
  975.3 13.9 reshape.337
  1009.2 85.8 %reduce-scatter.30.cloned.1.call-done = bf16[4640,128]{1,0:T(8,128)(2,1)} async-done(((bf16[37120,128]{1,0:T(8,128)(2,1)}), bf16[4640,128]{1,0:T(8,128)(2,1)}) %reduce-scatter.30.cloned.1.call-update) | async-done | bytes 1187856 | tf_op jit(solution)/shard_map/reduce_scatter | solution.py:104
  1095.1 100.9 %reduce-scatter.28.cloned.1.call-done = bf16[4640,128]{1,0:T(8,128)(2,1)} async-done(((bf16[37120,128]{1,0:T(8,128)(2,1)}), bf16[4640,128]{1,0:T(8,128)(2,1)}) %reduce-scatter.28.cloned.1.call-update) | async-done | bytes 1187856 | tf_op jit(solution)/shard_map/reduce_scatter | solution.py:101
  1197.4 77.0 %reduce-scatter.24.cloned.1.call-done = bf16[3488,128]{1,0:T(8,128)(2,1)} async-done(((bf16[27904,128]{1,0:T(8,128)(2,1)}), bf16[3488,128]{1,0:T(8,128)(2,1)}) %reduce-scatter.24.cloned.1.call-update) | async-done | bytes 892944 | tf_op jit(solution)/shard_map/reduce_scatter | solution.py:120
  1274.5 13.0 fusion.43
  1305.6 26.3 %reduce-scatter.32.cloned.1.call-done = bf16[32,128]{1,0:T(8,128)(2,1)} async-done(((bf16[256,128]{1,0:T(8,128)(2,1)}), bf16[32,128]{1,0:T(8,128)(2,1)}) %reduce-scatter.32.cloned.1.call-update) | async-done | bytes 8208 | tf_op jit(solution)/shard_map/reduce_scatter | solution.py:126
  1342.6 22.0 %reduce-scatter.40.cloned.1.call-done = bf16[1160,128]{1,0:T(8,128)(2,1)} async-done(((bf16[4640,128]{1,0:T(8,128)(2,1)}), bf16[1160,128]{1,0:T(8,128)(2,1)}) %reduce-scatter.40.cloned.1.call-update) | async-done | bytes 296976
  1366.5 32.9 %reduce-scatter.38.cloned.1.call-done = bf16[1160,128]{1,0:T(8,128)(2,1)} async-done(((bf16[4640,128]{1,0:T(8,128)(2,1)}), bf16[1160,128]{1,0:T(8,128)(2,1)}) %reduce-scatter.38.cloned.1.call-update) | async-done | bytes 296976
  1401.2 30.3 %reduce-scatter.34.cloned.1.call-done = bf16[872,128]{1,0:T(8,128)(2,1)} async-done(((bf16[3488,128]{1,0:T(8,128)(2,1)}), bf16[872,128]{1,0:T(8,128)(2,1)}) %reduce-scatter.34.cloned.1.call-update) | async-done | bytes 223248
  (343 shorter events, 478.2 us)
Async XLA Ops:
  7.2 35.9 %all-gather.17.cloned.1.call-start = ((), (), s32[]{:S(2)}) async-start(), calls=%async_computation.15 | async-start | bytes 1484800 | tf_op jit(solution)/shard_map/all_gather | solution.py:69
  7.9 64.9 %all-gather.21.cloned.1.call-start = ((), (), s32[]{:S(2)}) async-start(), calls=%async_computation.17 | async-start | bytes 1484800 | tf_op jit(solution)/shard_map/all_gather | solution.py:70
  8.7 138.0 %all-gather.9.cloned.1.call-start = ((), (), s32[]{:S(2)}) async-start(), calls=%async_computation.11 | async-start | bytes 8036352 | tf_op jit(solution)/shard_map/all_gather | solution.py:74
  28.0 44.9 %copy-start.54 = (bf16[8,128]{1,0:T(8,128)(2,1)S(1)}, bf16[8,128]{1,0:T(8,128)(2,1)}, u32[]{:S(2)}) copy-start(bf16[8,128]{1,0:T(8,128)(2,1)} %param.19) | copy-start | bytes 6148
  28.0 67.1 %copy-start.8 = (bf16[1,512,1088]{1,2,0:T(8,128)(2,1)S(1)}, bf16[1,512,1088]{1,2,0:T(8,128)(2,1)}, u32[]{:S(2)}) copy-start(bf16[1,512,1088]{1,2,0:T(8,128)(2,1)} %param.12) | copy-start | bytes 3342340
  28.0 152.3 %all-gather.15.cloned.1.call-start = ((), (), s32[]{:S(2)}) async-start(), calls=%async_computation.14 | async-start | bytes 2727936 | tf_op jit(solution)/shard_map/all_gather | solution.py:75
  38.4 232.2 %all-gather.19.cloned.1.call-start = ((), (), s32[]{:S(2)}) async-start(), calls=%async_computation.16 | async-start | bytes 10690560 | tf_op jit(solution)/shard_map/all_gather | solution.py:76
  43.1 318.8 %all-gather.23.cloned.1.call-start = ((), (), s32[]{:S(2)}) async-start(), calls=%async_computation.18 | async-start | bytes 10690560 | tf_op jit(solution)/shard_map/all_gather | solution.py:77
  72.8 344.2 %all-gather.13.cloned.1.call-start = ((), (), s32[]{:S(2)}) async-start(), calls=%async_computation.13 | async-start | bytes 5570560 | tf_op jit(solution)/shard_map/all_gather | solution.py:216
  95.3 70.9 %copy-start.36 = (f32[512]{0:T(512)}, f32[512]{0:T(512)S(1)}, u32[]{:S(2)}) copy-start(f32[512]{0:T(512)S(1)} %broadcast_multiply_fusion.1) | copy-start | bytes 6148
  96.2 69.9 %copy-start.40 = (f32[512]{0:T(512)}, f32[512]{0:T(512)S(1)}, u32[]{:S(2)}) copy-start(f32[512]{0:T(512)S(1)} %fusion.80) | copy-start | bytes 6148
  96.9 69.2 %copy-start.31 = (f32[1088]{0:T(1024)}, f32[1088]{0:T(1024)S(1)}, u32[]{:S(2)}) copy-start(f32[1088]{0:T(1024)S(1)} %get-tuple-element.315) | copy-start | bytes 13060
  96.9 69.2 %copy-start.49 = (f32[1088]{0:T(1024)}, f32[1088]{0:T(1024)S(1)}, u32[]{:S(2)}) copy-start(f32[1088]{0:T(1024)S(1)} %get-tuple-element.314) | copy-start | bytes 13060
  176.5 297.6 %all-gather.11.cloned.1.call-start = ((), (), s32[]{:S(2)}) async-start(), calls=%async_computation.12 | async-start | bytes 5570560 | tf_op jit(solution)/shard_map/all_gather | solution.py:215
  179.4 787.4 %reduce-scatter.22.cloned.1.call-start = ((), (), s32[]{:S(2)}) async-start(), calls=%async_computation.20 | async-start | bytes 5570560 | tf_op jit(solution)/shard_map/reduce_scatter | solution.py:317
  371.1 103.0 %copy-start.17 = (f32[17,512]{1,0:T(8,128)S(1)}, f32[17,512]{1,0:T(8,128)}, u32[]{:S(2)}) copy-start(f32[17,512]{1,0:T(8,128)} %custom-call.1) | copy-start | bytes 104452
  608.9 38.6 %copy-start.5 = (f32[512,1088]{0,1:T(8,128)}, f32[512,1088]{0,1:T(8,128)S(1)}, u32[]{:S(2)}) copy-start(f32[512,1088]{0,1:T(8,128)S(1)} %get-tuple-element.317) | copy-start | bytes 6684676
  608.9 38.5 %copy-start.29 = (f32[512]{0:T(512)}, f32[512]{0:T(512)S(1)}, u32[]{:S(2)}) copy-start(f32[512]{0:T(512)S(1)} %broadcast_multiply_fusion) | copy-start | bytes 6148
  609.3 38.2 %copy-start.34 = (f32[512]{0:T(512)}, f32[512]{0:T(512)S(1)}, u32[]{:S(2)}) copy-start(f32[512]{0:T(512)S(1)} %fusion.81) | copy-start | bytes 6148
  841.6 125.1 %reduce-scatter.20.cloned.1.call-start = ((), (), s32[]{:S(2)}) async-start(), calls=%async_computation.19 | async-start | bytes 5570560 | tf_op jit(solution)/shard_map/reduce_scatter | solution.py:314
  855.1 142.2 %reduce-scatter.26.cloned.1.call-start = ((), (), s32[]{:S(2)}) async-start(), calls=%async_computation.22 | async-start | bytes 2727936 | tf_op jit(solution)/shard_map/reduce_scatter | solution.py:123
  869.6 225.4 %reduce-scatter.30.cloned.1.call-start = ((), (), s32[]{:S(2)}) async-start(), calls=%async_computation.24 | async-start | bytes 10690560 | tf_op jit(solution)/shard_map/reduce_scatter | solution.py:104
  926.3 269.6 %reduce-scatter.28.cloned.1.call-start = ((), (), s32[]{:S(2)}) async-start(), calls=%async_computation.23 | async-start | bytes 10690560 | tf_op jit(solution)/shard_map/reduce_scatter | solution.py:101
  965.6 308.9 %reduce-scatter.24.cloned.1.call-start = ((), (), s32[]{:S(2)}) async-start(), calls=%async_computation.21 | async-start | bytes 8036352 | tf_op jit(solution)/shard_map/reduce_scatter | solution.py:120
  995.7 303.4 %reduce-scatter.36.cloned.1.call-start = ((), (), s32[]{:S(2)}) async-start(), calls=%async_computation.27 | async-start | bytes 378880
  997.3 334.6 %reduce-scatter.32.cloned.1.call-start = ((), (), s32[]{:S(2)}) async-start(), calls=%async_computation.25 | async-start | bytes 73728 | tf_op jit(solution)/shard_map/reduce_scatter | solution.py:126
  1007.3 188.9 %copy-start.55 = (u32[32]{0:T(128)S(1)}, u32[32]{0:T(128)}, u32[]{:S(2)}) copy-start(u32[32]{0:T(128)} %constant.112) | copy-start | bytes 388
  1008.3 266.1 %copy-start.6 = (f32[512,1088]{0,1:T(8,128)S(1)}, f32[512,1088]{0,1:T(8,128)}, u32[]{:S(2)}) copy-start(f32[512,1088]{0,1:T(8,128)} %copy-done.5) | copy-start | bytes 6684676
  1008.3 266.1 %copy-start.48 = (f32[1088]{0:T(1024)S(1)}, f32[1088]{0:T(1024)}, u32[]{:S(2)}) copy-start(f32[1088]{0:T(1024)} %get-tuple-element.309) | copy-start | bytes 13060
  1009.2 355.5 %reduce-scatter.40.cloned.1.call-start = ((), (), s32[]{:S(2)}) async-start(), calls=%async_computation.29 | async-start | bytes 1484800
  1095.0 304.3 %reduce-scatter.38.cloned.1.call-start = ((), (), s32[]{:S(2)}) async-start(), calls=%async_computation.28 | async-start | bytes 1484800
  1196.0 235.5 %reduce-scatter.34.cloned.1.call-start = ((), (), s32[]{:S(2)}) async-start(), calls=%async_computation.26 | async-start | bytes 1116160
  (56 other events, 239.0 us)
Sparse Core Ops, SparseCore 0:
  9.9 33.2 all-gather.16
  45.0 27.7 all-gather.20
  74.4 72.1 all-gather.8
  148.1 30.6 all-gather.14
  180.3 90.3 all-gather.18
  272.2 89.7 all-gather.22
  363.8 53.1 all-gather.12
  419.4 54.7 all-gather.10
  841.7 54.8 reduce-scatter.21
  899.5 54.8 reduce-scatter.19
  956.7 36.7 reduce-scatter.25
  995.8 99.1 reduce-scatter.29
  1097.4 98.4 reduce-scatter.27
  1198.2 76.1 reduce-scatter.23
  1277.2 21.9 reduce-scatter.35
  1301.8 30.0 reduce-scatter.31
  1335.0 29.6 reduce-scatter.39
  1367.7 31.5 reduce-scatter.37
  1402.7 28.7 reduce-scatter.33
where the time goes:
time: 1460 us; the launch traced here: 1440 us
  waiting for transfers between devices  708 us (48%)
  matrix products  324 us (22%)
  local copies, waits for them, and re-layouts  255 us (17%)
  other arithmetic  68.3 us (5%)
  blocking collectives  61.9 us (4%)
  between operations  15.4 us (1%)
    reduce_scatter x1, waiting for transfers between devices, reduce_mlp(): lax.psum_scatter(grad_up_flat.astype(jnp.bfloat16), 'dp', scatter_dimensi...  101 us
    unnamed x23, waiting for transfers between devices  98.4 us
    reduce_scatter x1, waiting for transfers between devices, reduce_mlp(): lax.psum_scatter(grad_down_flat.astype(jnp.bfloat16), 'dp', scatter_dimen...  85.8 us
    all_gather x1, waiting for transfers between devices, fetch_forward(): lax.all_gather(by_column[2], 'dp', axis=0, tiled=True)  85.5 us
    reduce_scatter x1, waiting for transfers between devices, reduce_attention(): lax.psum_scatter(grad_qkv_flat.astype(jnp.bfloat16), 'dp', scatter_dimens...  77 us
    dot_general x8, matrix products, visible_scores(): jnp.einsum('qhd,khd->hqk', query_heads, key_heads, preferred_element_type...  65.2 us
    all_gather x1, waiting for transfers between devices, fetch_forward(): lax.all_gather(by_column[3], 'dp', axis=0, tiled=True)  64.1 us
    reshape x4, local copies, waits for them, and re-layouts, to_flat(): flat_values = grad_matrix.reshape(-1)  58 us
  transfers between devices with their start and end apart: 19, of which 15 were waited for; matrix products, arithmetic and copies ran while one was open for 19% of the time, Pallas kernels for 0%

commit v1 on v0

v1 whole, which is shorter than its diff:
```python
import jax
import jax.numpy as jnp
from jax import lax
from jax.experimental import pallas as pl
from jax.experimental.pallas import tpu as pltpu
from jax.sharding import PartitionSpec as P

HEADS = 17
FF = 4352


eps_norm = 1e-05
masked_score = -1e30


def layer_norm(values, gain_vec, shift_vec):
    centre = jnp.mean(values, axis=-1, keepdims=True)
    centred = values - centre
    spread = jnp.mean(centred * centred, axis=-1, keepdims=True)
    return centred * lax.rsqrt(spread + eps_norm) * gain_vec + shift_vec


def unpack(flat_values, model_width, hidden_units):
    gain_one = flat_values[0:model_width]
    shift_one = flat_values[model_width : 2 * model_width]
    bias_query = flat_values[2 * model_width : 3 * model_width]
    bias_value = flat_values[3 * model_width : 4 * model_width]
    bias_proj = flat_values[4 * model_width : 5 * model_width]
    gain_two = flat_values[5 * model_width : 6 * model_width]
    shift_two = flat_values[6 * model_width : 7 * model_width]
    bias_up = flat_values[7 * model_width : 7 * model_width + hidden_units]
    bias_down = flat_values[7 * model_width + hidden_units : 8 * model_width + hidden_units]
    return (
        gain_one,
        shift_one,
        bias_query,
        bias_value,
        bias_proj,
        gain_two,
        shift_two,
        bias_up,
        bias_down,
    )


def take_matrix(flat_rows, row_count, col_count):
    return flat_rows.reshape(-1)[: row_count * col_count].reshape(row_count, col_count)


def to_flat(grad_matrix, row_count):
    flat_values = grad_matrix.reshape(-1)
    return jnp.pad(flat_values, (0, row_count * 128 - flat_values.shape[0])).reshape(row_count, 128)


def shape_weights(gathered, model_width):
    return (
        take_matrix(gathered[0], model_width, 3 * model_width),
        take_matrix(gathered[1], model_width, model_width),
        take_matrix(gathered[2], model_width, FF),
        take_matrix(gathered[3], FF, model_width),
        gathered[4],
    )


def fetch(*flat_weights):
    return tuple(lax.all_gather(flat, ("dp", "seq"), axis=0, tiled=True) for flat in flat_weights)


def reduce_mlp(grad_up_flat, grad_down_flat):
    by_row = (
        lax.psum_scatter(
            grad_up_flat.astype(jnp.bfloat16), "dp", scatter_dimension=0, tiled=True
        ).astype(jnp.float32),
        lax.psum_scatter(
            grad_down_flat.astype(jnp.bfloat16), "dp", scatter_dimension=0, tiled=True
        ).astype(jnp.float32),
    )
    return (
        lax.psum_scatter(
            by_row[0].astype(jnp.bfloat16), "seq", scatter_dimension=0, tiled=True
        ).astype(jnp.float32),
        lax.psum_scatter(
            by_row[1].astype(jnp.bfloat16), "seq", scatter_dimension=0, tiled=True
        ).astype(jnp.float32),
    )


def reduce_attention(grad_qkv_flat, grad_out_flat, grad_vec_flat):
    by_row = (
        lax.psum_scatter(
            grad_qkv_flat.astype(jnp.bfloat16), "dp", scatter_dimension=0, tiled=True
        ).astype(jnp.float32),
        lax.psum_scatter(
            grad_out_flat.astype(jnp.bfloat16), "dp", scatter_dimension=0, tiled=True
        ).astype(jnp.float32),
        lax.psum_scatter(
            grad_vec_flat.astype(jnp.bfloat16), "dp", scatter_dimension=0, tiled=True
        ).astype(jnp.float32),
    )
    return (
        lax.psum_scatter(
            by_row[0].astype(jnp.bfloat16), "seq", scatter_dimension=0, tiled=True
        ).astype(jnp.float32),
        lax.psum_scatter(
            by_row[1].astype(jnp.bfloat16), "seq", scatter_dimension=0, tiled=True
        ).astype(jnp.float32),
        lax.psum_scatter(
            by_row[2].astype(jnp.bfloat16), "seq", scatter_dimension=0, tiled=True
        ).astype(jnp.float32),
    )


KEY_TILE = 256
LANES = 128


def contract(left, right, left_dim, right_dim):
    return lax.dot_general(
        left, right, (((left_dim,), (right_dim,)), ((), ())), preferred_element_type=jnp.float32
    )


def stack_pair(block):
    half = block.shape[1] // 2
    lane = lax.broadcasted_iota(jnp.int32, block.shape, 1)
    zero = jnp.zeros_like(block)
    return jnp.concatenate(
        [jnp.where(lane < half, block, zero), jnp.where(lane < half, zero, block)], axis=0
    )


def unstack_pair(wide, rows):
    half = wide.shape[0] // 2
    return jnp.concatenate([wide[:half, :rows], wide[half:, rows:]], axis=0)


def masked_scores(bounds_ref, keys, stacked, starts, places, offset):
    scores = contract(keys, stacked, 1, 1)
    key_places = offset + lax.broadcasted_iota(jnp.int32, scores.shape, 0)
    visible = (key_places >= starts) & (key_places <= places)
    return jnp.where(visible, scores, masked_score)


def forward_kernel(
    bounds_ref, q_ref, k_ref, v_ref, starts_ref, places_ref, o_ref, lse_ref, top, total, acc
):
    rows = q_ref.shape[0]
    stacked = stack_pair(q_ref[...])
    starts = starts_ref[...]
    places = places_ref[...]
    top[...] = jnp.full_like(top, masked_score)
    total[...] = jnp.zeros_like(total)
    acc[...] = jnp.zeros_like(acc)

    def step(tile, carry):
        offset = pl.multiple_of(tile * KEY_TILE, KEY_TILE)
        keys = k_ref[pl.ds(offset, KEY_TILE), :]
        values = v_ref[pl.ds(offset, KEY_TILE), :]
        scores = masked_scores(bounds_ref, keys, stacked, starts, places, offset)
        old_top = top[...]
        new_top = jnp.maximum(old_top, jnp.max(scores, axis=0, keepdims=True))
        weights = jnp.exp(scores - new_top)
        factor = jnp.exp(old_top - new_top)
        top[...] = new_top
        total[...] = total[...] * factor + jnp.sum(weights, axis=0, keepdims=True)
        acc[...] = acc[...] * factor + contract(values, weights.astype(jnp.bfloat16), 0, 0)
        return carry

    lax.fori_loop(bounds_ref[0], bounds_ref[1], step, 0)
    lse_ref[0] = top[...] + jnp.log(total[...])
    o_ref[...] = unstack_pair(acc[...] / total[...], rows).T


def backward_kernel(
    bounds_ref, q_ref, k_ref, v_ref, g_ref, o_ref, lse_ref, starts_ref, places_ref,
    dq_ref, dk_ref, dv_ref, acc,
):
    rows = q_ref.shape[0]
    stacked = stack_pair(q_ref[...])
    grads = g_ref[...]
    stacked_g = stack_pair(grads)
    mixed = (grads.astype(jnp.float32) * o_ref[...]).T
    half = mixed.shape[0] // 2
    row_dots = jnp.concatenate(
        [
            jnp.sum(mixed[:half], axis=0, keepdims=True),
            jnp.sum(mixed[half:], axis=0, keepdims=True),
        ],
        axis=1,
    )
    starts = starts_ref[...]
    places = places_ref[...]
    totals = lse_ref[0]
    acc[...] = jnp.zeros_like(acc)
    dk_ref[...] = jnp.zeros_like(dk_ref)
    dv_ref[...] = jnp.zeros_like(dv_ref)

    def step(tile, carry):
        offset = pl.multiple_of(tile * KEY_TILE, KEY_TILE)
        keys = k_ref[pl.ds(offset, KEY_TILE), :]
        values = v_ref[pl.ds(offset, KEY_TILE), :]
        scores = masked_scores(bounds_ref, keys, stacked, starts, places, offset)
        probs = jnp.exp(scores - totals)
        d_probs = contract(values, stacked_g, 1, 1)
        d_scores = (probs * (d_probs - row_dots)).astype(jnp.bfloat16)
        dv_ref[pl.ds(offset, KEY_TILE), :] = contract(
            probs.astype(jnp.bfloat16), stacked_g, 1, 0
        ).astype(dv_ref.dtype)
        dk_ref[pl.ds(offset, KEY_TILE), :] = contract(d_scores, stacked, 1, 0).astype(dk_ref.dtype)
        acc[...] += contract(keys, d_scores, 0, 0)
        return carry

    lax.fori_loop(bounds_ref[0], bounds_ref[1], step, 0)
    dq_ref[...] = unstack_pair(acc[...], rows).T


def column_spec(rows):
    return pl.BlockSpec((rows, LANES), lambda pair, bounds: (0, pair))


def whole_spec(cols):
    return pl.BlockSpec((1, cols), lambda pair, bounds: (0, 0))


def pair_spec(cols):
    return pl.BlockSpec((1, 1, cols), lambda pair, bounds: (pair, 0, 0))


def attend(bounds, queries, keys, values, starts, places):
    rows, width = queries.shape
    length = keys.shape[0]
    pairs = width // LANES
    return pl.pallas_call(
        forward_kernel,
        grid_spec=pltpu.PrefetchScalarGridSpec(
            num_scalar_prefetch=1,
            grid=(pairs,),
            in_specs=[
                column_spec(rows), column_spec(length), column_spec(length),
                whole_spec(2 * rows), whole_spec(2 * rows),
            ],
            out_specs=[column_spec(rows), pair_spec(2 * rows)],
            scratch_shapes=[
                pltpu.VMEM((1, 2 * rows), jnp.float32),
                pltpu.VMEM((1, 2 * rows), jnp.float32),
                pltpu.VMEM((LANES, 2 * rows), jnp.float32),
            ],
        ),
        out_shape=[
            jax.ShapeDtypeStruct((rows, width), jnp.float32),
            jax.ShapeDtypeStruct((pairs, 1, 2 * rows), jnp.float32),
        ],
        compiler_params=pltpu.CompilerParams(vmem_limit_bytes=40 * 1024 * 1024),
        cost_estimate=pl.CostEstimate(
            flops=8 * rows * length * width, bytes_accessed=8 * length * width,
            transcendentals=rows * length * width // 64,
        ),
        name="attention_forward",
    )(bounds, queries, keys, values, starts, places)


def attend_back(bounds, queries, keys, values, grads, mixed, totals, starts, places):
    rows, width = queries.shape
    length = keys.shape[0]
    pairs = width // LANES
    return pl.pallas_call(
        backward_kernel,
        grid_spec=pltpu.PrefetchScalarGridSpec(
            num_scalar_prefetch=1,
            grid=(pairs,),
            in_specs=[
                column_spec(rows), column_spec(length), column_spec(length),
                column_spec(rows), column_spec(rows), pair_spec(2 * rows),
                whole_spec(2 * rows), whole_spec(2 * rows),
            ],
            out_specs=[column_spec(rows), column_spec(length), column_spec(length)],
            scratch_shapes=[pltpu.VMEM((LANES, 2 * rows), jnp.float32)],
        ),
        out_shape=[
            jax.ShapeDtypeStruct((rows, width), jnp.float32),
            jax.ShapeDtypeStruct((length, width), jnp.bfloat16),
            jax.ShapeDtypeStruct((length, width), jnp.bfloat16),
        ],
        compiler_params=pltpu.CompilerParams(vmem_limit_bytes=48 * 1024 * 1024),
        cost_estimate=pl.CostEstimate(
            flops=20 * rows * length * width, bytes_accessed=12 * length * width,
            transcendentals=rows * length * width // 64,
        ),
        name="attention_backward",
    )(bounds, queries, keys, values, grads, mixed, totals, starts, places)


def body(hidden_in, segments, cotangent, w_qkv, w_out, w_up, w_down, vectors):
    tok_rows = hidden_in.shape[1]
    model_width = hidden_in.shape[2]
    head_dim = model_width // HEADS
    score_scale = head_dim ** (-0.5)
    length = segments.shape[1]
    spread_count = lax.axis_size("dp") * lax.axis_size("seq")
    seg_row = segments[0]
    query_first = lax.axis_index("seq") * tok_rows
    query_places = query_first + jnp.arange(tok_rows, dtype=jnp.int32)
    query_segs = lax.dynamic_slice_in_dim(seg_row, query_first, tok_rows)
    fwd_gathered = fetch(w_qkv, w_out, w_up, w_down, vectors)
    fwd_weights = shape_weights(fwd_gathered, model_width)
    hidden_units = FF
    (
        gain_one,
        shift_one,
        bias_query,
        bias_value,
        bias_proj,
        gain_two,
        shift_two,
        bias_up,
        bias_down,
    ) = unpack(fwd_weights[4].reshape(-1).astype(jnp.float32), model_width, hidden_units)
    tokens = hidden_in[0].astype(jnp.float32)
    normed_f, pull_one = jax.vjp(layer_norm, tokens, gain_one, shift_one)
    normed = normed_f.astype(jnp.bfloat16)
    packed = jnp.dot(normed, fwd_weights[0], preferred_element_type=jnp.float32)
    queries = (packed[:, :model_width] + bias_query).astype(jnp.bfloat16)
    key_rows = packed[:, model_width : 2 * model_width].astype(jnp.bfloat16)
    value_rows = (packed[:, 2 * model_width :] + bias_value).astype(jnp.bfloat16)
    pair_width = pl.cdiv(model_width, LANES) * LANES

    def widen(matrix):
        return jnp.pad(matrix, ((0, 0), (0, pair_width - matrix.shape[1])))

    queries = widen(queries * jnp.bfloat16(score_scale))
    key_rows = widen(key_rows)
    value_rows = widen(value_rows)
    query_starts = jnp.sum(
        (seg_row[None, :] < query_segs[:, None]).astype(jnp.int32), axis=1, dtype=jnp.int32
    )
    bounds = jnp.stack([query_starts[0] // KEY_TILE, pl.cdiv(query_first + tok_rows, KEY_TILE)])
    starts = jnp.tile(query_starts, 2)[None]
    places = jnp.tile(query_places, 2)[None]
    key_all = lax.all_gather(key_rows, "seq", axis=0, tiled=True)
    value_all = lax.all_gather(value_rows, "seq", axis=0, tiled=True)
    attended_f, log_total = attend(bounds, queries, key_all, value_all, starts, places)
    attended = attended_f[:, :model_width].astype(jnp.bfloat16)
    middle = (
        tokens + jnp.dot(attended, fwd_weights[1], preferred_element_type=jnp.float32) + bias_proj
    )
    normed_two_f, pull_two = jax.vjp(layer_norm, middle, gain_two, shift_two)
    normed_two = normed_two_f.astype(jnp.bfloat16)
    before = jnp.dot(normed_two, fwd_weights[2], preferred_element_type=jnp.float32) + bias_up
    active_f, pull_gelu = jax.vjp(jax.nn.gelu, before)
    active = active_f.astype(jnp.bfloat16)
    result = (
        middle + jnp.dot(active, fwd_weights[3], preferred_element_type=jnp.float32) + bias_down
    )
    hidden_out = result.astype(jnp.bfloat16)[None]
    back_weights = fwd_weights
    cot_rows = cotangent[0]
    cot_float = cot_rows.astype(jnp.float32)
    grad_down_full = jnp.dot(active.T, cot_rows, preferred_element_type=jnp.float32)
    d_bias_down = jnp.sum(cot_float, axis=0)
    d_active = jnp.dot(cot_rows, back_weights[3].T, preferred_element_type=jnp.float32)
    d_before = pull_gelu(d_active)[0].astype(jnp.bfloat16)
    d_bias_up = jnp.sum(d_before.astype(jnp.float32), axis=0)
    grad_up_full = jnp.dot(normed_two.T, d_before, preferred_element_type=jnp.float32)
    d_normed_two = jnp.dot(d_before, back_weights[2].T, preferred_element_type=jnp.float32)
    d_middle_norm, d_gain_two, d_shift_two = pull_two(d_normed_two)
    d_middle = cot_float + d_middle_norm
    mlp_grads = reduce_mlp(
        to_flat(grad_up_full, w_up.shape[0] * spread_count),
        to_flat(grad_down_full, w_down.shape[0] * spread_count),
    )
    d_proj = d_middle.astype(jnp.bfloat16)
    d_bias_proj = jnp.sum(d_middle, axis=0)
    grad_out_full = jnp.dot(attended.T, d_proj, preferred_element_type=jnp.float32)
    d_attended = jnp.dot(d_proj, back_weights[1].T, preferred_element_type=jnp.float32).astype(
        jnp.bfloat16
    )
    dq_sum, key_terms, value_terms = attend_back(
        bounds, queries, key_all, value_all, widen(d_attended), attended_f, log_total, starts,
        places,
    )
    d_key = lax.psum_scatter(key_terms, "seq", scatter_dimension=0, tiled=True)[:, :model_width]
    d_value = lax.psum_scatter(value_terms, "seq", scatter_dimension=0, tiled=True)[:, :model_width]
    d_query = (score_scale * dq_sum[:, :model_width]).astype(jnp.bfloat16)
    d_packed = jnp.concatenate([d_query, d_key, d_value], axis=1)
    grad_qkv_full = jnp.dot(normed.T, d_packed, preferred_element_type=jnp.float32)
    d_normed = jnp.dot(d_packed, back_weights[0].T, preferred_element_type=jnp.float32)
    d_tokens_norm, d_gain_one, d_shift_one = pull_one(d_normed)
    grad_in = (d_middle + d_tokens_norm)[None]
    vector_grads = jnp.concatenate(
        [
            d_gain_one,
            d_shift_one,
            jnp.sum(d_query.astype(jnp.float32), axis=0),
            jnp.sum(d_value.astype(jnp.float32), axis=0),
            d_bias_proj,
            d_gain_two,
            d_shift_two,
            d_bias_up,
            d_bias_down,
        ]
    )
    attn_grads = reduce_attention(
        to_flat(grad_qkv_full, w_qkv.shape[0] * spread_count),
        to_flat(grad_out_full, w_out.shape[0] * spread_count),
        to_flat(vector_grads, vectors.shape[0] * spread_count),
    )
    return (
        hidden_out,
        grad_in,
        attn_grads[0],
        attn_grads[1],
        mlp_grads[0],
        mlp_grads[1],
        attn_grads[2],
    )


def solution(mesh):
    return jax.shard_map(
        body,
        mesh=mesh,
        in_specs=(
            P("dp", "seq", None),
            P("dp", None),
            P("dp", "seq", None),
            P(("dp", "seq"), None),
            P(("dp", "seq"), None),
            P(("dp", "seq"), None),
            P(("dp", "seq"), None),
            P(("dp", "seq"), None),
        ),
        out_specs=(
            P("dp", "seq", None),
            P("dp", "seq", None),
            P(("dp", "seq"), None),
            P(("dp", "seq"), None),
            P(("dp", "seq"), None),
            P(("dp", "seq"), None),
            P(("dp", "seq"), None),
        ),
        check_vma=False,
    )
```

time: 1460 us -> 1200 us (0.82)
  matrix products: 324 us -> 105 us
  other arithmetic: 68.3 us -> 21.5 us
  Pallas kernels: 0 us -> 43.4 us
  local copies, waits for them, and re-layouts: 255 us -> 219 us
  blocking collectives: 61.9 us -> 81.3 us
    dot_general x28 -> x0, matrix products: 216 us -> none  [the longest x8 65.2 us: visible_scores(): jnp.einsum('qhd,khd->hqk', query_heads, key_heads, preferred_element_type...]
    all_gather x6 -> x4, waiting for transfers between devices: 234 us -> 147 us  [fetch(): lax.all_gather(flat, ('dp', 'seq'), axis=0, tiled=True)]
    reduce_scatter x2, waiting for transfers between devices: 0.01 us -> 65.4 us  [the longest x1 58.6 us: body(): lax.psum_scatter(key_terms, 'seq', scatter_dimension=0, tiled=True)]
    pallas_call x0 -> x2, Pallas kernels: none -> 43.4 us  [the longest x1 25 us: attend_back(): pl.pallas_call(backward_kernel, grid_spec=pltpu.PrefetchScalarGridSpec(nu...]
    reduce_sum x4 -> x1, other arithmetic: 41 us -> 0.59 us  [body(): jnp.sum((seg_row[None, :] < query_segs[:, None]).astype(jnp.int32), axis=...]
    all_gather x1, waiting for transfers between devices: 28.7 us -> 59.4 us  [body(): value_all = lax.all_gather(value_rows, 'seq', axis=0, tiled=True)]
    dynamic_slice x28 -> x0, local copies, waits for them, and re-layouts: 27.2 us -> none  [the longest x4 9.61 us: back_block(): lax.dynamic_slice_in_dim(back_values, offset, block_rows)]
    all_gather x1, waiting for transfers between devices: 57.2 us -> 30.3 us  [body(): key_all = lax.all_gather(key_rows, 'seq', axis=0, tiled=True)]
  transfers between devices with their start and end apart: 19 -> 17, of which waited for: 15 -> 17; matrix products, arithmetic and copies ran while one was open for 19% -> 24% of each run, Pallas kernels for 0% -> 0%
where the time goes in v1:
time: 1200 us; the launch traced here: 1190 us
  waiting for transfers between devices  698 us (58%)
  local copies, waits for them, and re-layouts  219 us (18%)
  matrix products  105 us (9%)
  blocking collectives  81.3 us (7%)
  Pallas kernels  43.4 us (4%)
  other arithmetic  21.5 us (2%)
  between operations  18.1 us (2%)
    all_gather x4, waiting for transfers between devices, fetch(): lax.all_gather(flat, ('dp', 'seq'), axis=0, tiled=True)  147 us
    reduce_scatter x1, waiting for transfers between devices, reduce_mlp(): lax.psum_scatter(grad_down_flat.astype(jnp.bfloat16), 'dp', scatter_dimen...  101 us
    unnamed x21, waiting for transfers between devices  100 us
    reduce_scatter x1, waiting for transfers between devices, reduce_mlp(): lax.psum_scatter(grad_up_flat.astype(jnp.bfloat16), 'dp', scatter_dimensi...  89.6 us
    reduce_scatter x1, waiting for transfers between devices, reduce_attention(): lax.psum_scatter(grad_qkv_flat.astype(jnp.bfloat16), 'dp', scatter_dimens...  77.2 us
    all_gather x1, blocking collectives, fetch(): lax.all_gather(flat, ('dp', 'seq'), axis=0, tiled=True)  71.1 us
    all_gather x1, waiting for transfers between devices, body(): value_all = lax.all_gather(value_rows, 'seq', axis=0, tiled=True)  59.4 us
    reduce_scatter x1, waiting for transfers between devices, body(): lax.psum_scatter(key_terms, 'seq', scatter_dimension=0, tiled=True)  58.6 us
  transfers between devices with their start and end apart: 17, of which 17 were waited for; matrix products, arithmetic and copies ran while one was open for 24% of the time, Pallas kernels for 0%

profile of v1, /device:TPU:0, one launch (start us, length us, event | category | flops | bytes accessed | tf_op | source)
XLA Modules:
  0.0 1188.2 jit_solution(14847096087180408462)
XLA Ops:
  10.0 71.1 %all_gather.21 = bf16[256,128]{1,0:T(8,128)(2,1)S(1)} all-gather(bf16[8,128]{1,0:T(8,128)(2,1)} %param.15), channel_id=1, replica_groups=mesh['dp'=8,'seq'=4] {'dp','seq'}, dimensions={0}, use_global_device_ids=true | all-gather | bytes 67584 | tf_op jit(solution)/shard_map/all_gather | solution.py:66
  92.9 13.1 %reshape.172 = bf16[1088,3264]{1,0:T(8,128)(2,1)} reshape(bf16[27744,128]{1,0:T(8,128)(2,1)} %slice.92) | data formatting | bytes 14204928 | tf_op jit(solution)/shard_map/reshape | solution.py:47
  131.2 14.4 %all-gather.13.cloned.1.call-done = bf16[9472,128]{1,0:T(8,128)(2,1)} async-done(((bf16[296,128]{1,0:T(8,128)(2,1)}), bf16[9472,128]{1,0:T(8,128)(2,1)}) %all-gather.13.cloned.1.call-update) | async-done | bytes 2424848 | tf_op jit(solution)/shard_map/all_gather | solution.py:66
  156.0 73.3 %all-gather.17.cloned.1.call-done = bf16[37120,128]{1,0:T(8,128)(2,1)} async-done(((bf16[1160,128]{1,0:T(8,128)(2,1)}), bf16[37120,128]{1,0:T(8,128)(2,1)}) %all-gather.17.cloned.1.call-update) | async-done | bytes 9502736 | tf_op jit(solution)/shard_map/all_gather | solution.py:66
  238.5 17.1 %reshape.175 = bf16[4352,1088]{1,0:T(8,128)(2,1)} reshape(bf16[36992,128]{1,0:T(8,128)(2,1)} %slice.105) | data formatting | bytes 18939904 | tf_op jit(solution)/shard_map/reshape | solution.py:47
  255.6 57.1 %all-gather.15.cloned.1.call-done = bf16[37120,128]{1,0:T(8,128)(2,1)} async-done(((bf16[1160,128]{1,0:T(8,128)(2,1)}), bf16[37120,128]{1,0:T(8,128)(2,1)}) %all-gather.15.cloned.1.call-update) | async-done | bytes 9502736 | tf_op jit(solution)/shard_map/all_gather | solution.py:66
  312.7 9.2 slice.103
  321.9 17.9 %reshape.174 = bf16[1088,4352]{1,0:T(8,128)(2,1)} reshape(bf16[36992,128]{1,0:T(8,128)(2,1)} %slice.103) | data formatting | bytes 18939904 | tf_op jit(solution)/shard_map/reshape | solution.py:47
  339.8 30.3 %all-gather.9.cloned.1.call-done.k_ref = bf16[2048,1152]{1,0:T(8,128)(2,1)} async-done(((bf16[512,1152]{1,0:T(8,128)(2,1)}), bf16[2048,1152]{1,0:T(8,128)(2,1)}) %all-gather.9.cloned.1.call-update) | async-done | bytes 4718608 | tf_op jit(solution)/shard_map/all_gather | solution.py:339
  370.1 59.4 %all-gather.11.cloned.1.call-done.v_ref = bf16[2048,1152]{1,0:T(8,128)(2,1)} async-done(((bf16[512,1152]{1,0:T(8,128)(2,1)}), bf16[2048,1152]{1,0:T(8,128)(2,1)}) %all-gather.11.cloned.1.call-update) | async-done | bytes 4718608 | tf_op jit(solution)/shard_map/all_gather | solution.py:340
  434.1 18.4 %attention_forward.1 = (f32[512,1152]{1,0:T(8,128)S(1)}, f32[9,1,1024]{2,1,0:T(1,128)S(1)}) custom-call(s32[2]{0:T(128)S(1)} %pad_add_fusion.bounds_ref, bf16[512,1152]{1,0:T(8,128)(2,1)S(1)} %pad.37.q_ref, bf16[2048,1152]{1,0:T(8,128)(2,1)S(1)} %copy-done, bf16[2048,1152]{1,0:T(8,128)(2,1)S(1)} %copy-done.1, s32[1,1024]{1,0:T(1,128)S(1)} %bitcast.100, ...), custom_call_target="tpu_custom_call" | custom-call | flops 9663676416 | bytes 18874368 | tf_op jit(solution)/shard_map/attention_forward/pallas_call | solution.py:233
  466.9 16.4 %fusion.57 = (bf16[4352]{0:T(1024)(128)(2,1)}, bf16[512,4352]{1,0:T(8,128)(2,1)}) fusion(f32[512,4352]{1,0:T(8,128)} %fusion.50, f32[4352]{0:T(1024)S(1)} %copy-done.29, bf16[4352,1088]{1,0:T(8,128)(2,1)} %reshape.175, bf16[1,512,1088]{1,2,0:T(8,128)(2,1)S(1)} %copy-done.11), kind=kOutput, calls=%fused_computation.101 | convolution fusion | flops 4897632256 | bytes 23979520 | tf_op jit(solution)/shard_map/dot_general | solution.py:360
  499.2 25.0 %attention_backward.1 = (f32[512,1152]{1,0:T(8,128)S(1)}, bf16[2048,1152]{1,0:T(8,128)(2,1)}, bf16[2048,1152]{1,0:T(8,128)(2,1)}) custom-call(s32[2]{0:T(128)S(1)} %pad_add_fusion.bounds_ref, bf16[512,1152]{1,0:T(8,128)(2,1)S(1)} %pad.37.q_ref, bf16[2048,1152]{1,0:T(8,128)(2,1)} %all-gather.9.cloned.1.call-done.k_ref, ...), custom_call_target="tpu_custom_call" | custom-call | flops 24159191040 | bytes 28311552 | tf_op jit(solution)/shard_map/attention_backward/pallas_call | solution.py:266
  539.9 10.3 convolution_convert_fusion.1
  550.2 18.3 %reshape.178 = bf16[4734976]{0:T(1024)(128)(2,1)} reshape(bf16[1088,4352]{1,0:T(8,128)(2,1)} %convolution_convert_fusion.1) | data formatting | bytes 18939904 | tf_op jit(solution)/shard_map/reshape | solution.py:51
  568.5 9.2 pad_bitcast_fusion.1
  579.0 12.4 %convolution_convert_fusion = bf16[4352,1088]{0,1:T(8,128)(2,1)} fusion(bf16[1,512,1088]{1,2,0:T(8,128)(2,1)S(1)} %copy-done.12, f32[512,4352]{1,0:T(8,128)} %fusion.50, f32[4352]{0:T(1024)S(1)} %copy-done.30), kind=kOutput, calls=%fused_computation | convolution fusion | flops 4875632640 | bytes 19514368 | tf_op jit(solution)/shard_map/dot_general | solution.py:358
  591.4 14.1 %copy.38 = bf16[4352,1088]{1,0:T(8,128)(2,1)} copy(bf16[4352,1088]{0,1:T(8,128)(2,1)} %convolution_convert_fusion) | data formatting | bytes 18939904 | tf_op jit(solution)/shard_map/convert.14
  605.5 19.5 %reshape.179 = bf16[4734976]{0:T(1024)(128)(2,1)} reshape(bf16[4352,1088]{1,0:T(8,128)(2,1)} %copy.38) | data formatting | bytes 18939904 | tf_op jit(solution)/shard_map/reshape | solution.py:51
  625.0 9.3 pad_bitcast_fusion
  644.1 58.6 %reduce-scatter.20.cloned.1.call-done = bf16[512,1152]{1,0:T(8,128)(2,1)} async-done(((bf16[2048,1152]{1,0:T(8,128)(2,1)}), bf16[512,1152]{1,0:T(8,128)(2,1)}) %reduce-scatter.20.cloned.1.call-update) | async-done | bytes 1179664 | tf_op jit(solution)/shard_map/reduce_scatter | solution.py:381
  717.9 13.9 %reshape.176 = bf16[3551232]{0:T(1024)(128)(2,1)} reshape(bf16[1088,3264]{1,0:T(8,128)(2,1)} %convolution_convert_fusion.2) | data formatting | bytes 14204928 | tf_op jit(solution)/shard_map/reshape | solution.py:51
  753.6 89.6 %reduce-scatter.28.cloned.1.call-done = bf16[4640,128]{1,0:T(8,128)(2,1)} async-done(((bf16[37120,128]{1,0:T(8,128)(2,1)}), bf16[4640,128]{1,0:T(8,128)(2,1)}) %reduce-scatter.28.cloned.1.call-update) | async-done | bytes 1187856 | tf_op jit(solution)/shard_map/reduce_scatter | solution.py:71
  843.4 100.9 %reduce-scatter.30.cloned.1.call-done = bf16[4640,128]{1,0:T(8,128)(2,1)} async-done(((bf16[37120,128]{1,0:T(8,128)(2,1)}), bf16[4640,128]{1,0:T(8,128)(2,1)}) %reduce-scatter.30.cloned.1.call-update) | async-done | bytes 1187856 | tf_op jit(solution)/shard_map/reduce_scatter | solution.py:74
  945.5 77.2 %reduce-scatter.24.cloned.1.call-done = bf16[3488,128]{1,0:T(8,128)(2,1)} async-done(((bf16[27904,128]{1,0:T(8,128)(2,1)}), bf16[3488,128]{1,0:T(8,128)(2,1)}) %reduce-scatter.24.cloned.1.call-update) | async-done | bytes 892944 | tf_op jit(solution)/shard_map/reduce_scatter | solution.py:90
  1022.8 13.0 %fusion.15 = bf16[1,512,1088]{1,2,0:T(8,128)(2,1)} fusion(f32[512,1088]{0,1:T(8,128)S(1)} %copy-done.6, bf16[4352,1088]{1,0:T(8,128)(2,1)} %reshape.175, f32[1088]{0:T(1024)S(1)} %copy-done.40, f32[512,4352]{1,0:T(8,128)} %fusion.50, f32[4352]{0:T(1024)S(1)} %copy-done.30), kind=kOutput, calls=%fused_computation.34 | convolution fusion | flops 4872568832 | bytes 21746944 | tf_op jit(solution)/shard_map/dot_general | solution.py:352
  1035.8 11.7 reduce-scatter.36.cloned.1.call-done
  1054.0 26.2 %reduce-scatter.32.cloned.1.call-done = bf16[32,128]{1,0:T(8,128)(2,1)} async-done(((bf16[256,128]{1,0:T(8,128)(2,1)}), bf16[32,128]{1,0:T(8,128)(2,1)}) %reduce-scatter.32.cloned.1.call-update) | async-done | bytes 8208 | tf_op jit(solution)/shard_map/reduce_scatter | solution.py:96
  1080.3 10.2 all-reduce.13
  1091.1 22.0 %reduce-scatter.38.cloned.1.call-done = bf16[1160,128]{1,0:T(8,128)(2,1)} async-done(((bf16[4640,128]{1,0:T(8,128)(2,1)}), bf16[1160,128]{1,0:T(8,128)(2,1)}) %reduce-scatter.38.cloned.1.call-update) | async-done | bytes 296976
  1114.9 32.9 %reduce-scatter.40.cloned.1.call-done = bf16[1160,128]{1,0:T(8,128)(2,1)} async-done(((bf16[4640,128]{1,0:T(8,128)(2,1)}), bf16[1160,128]{1,0:T(8,128)(2,1)}) %reduce-scatter.40.cloned.1.call-update) | async-done | bytes 296976
  1149.6 30.1 %reduce-scatter.34.cloned.1.call-done = bf16[872,128]{1,0:T(8,128)(2,1)} async-done(((bf16[3488,128]{1,0:T(8,128)(2,1)}), bf16[872,128]{1,0:T(8,128)(2,1)}) %reduce-scatter.34.cloned.1.call-update) | async-done | bytes 223248
  (204 shorter events, 167.8 us)
Async XLA Ops:
  7.2 75.4 %copy-start.8 = (bf16[1,512,1088]{1,2,0:T(8,128)(2,1)S(1)}, bf16[1,512,1088]{1,2,0:T(8,128)(2,1)}, u32[]{:S(2)}) copy-start(bf16[1,512,1088]{1,2,0:T(8,128)(2,1)} %param.8) | copy-start | bytes 3342340
  7.2 79.4 %all-gather.7.cloned.1.call-start = ((), (), s32[]{:S(2)}) async-start(), calls=%async_computation.11 | async-start | bytes 7366656 | tf_op jit(solution)/shard_map/all_gather | solution.py:66
  7.9 137.7 %all-gather.13.cloned.1.call-start = ((), (), s32[]{:S(2)}) async-start(), calls=%async_computation.14 | async-start | bytes 2500608 | tf_op jit(solution)/shard_map/all_gather | solution.py:66
  8.7 220.7 %all-gather.17.cloned.1.call-start = ((), (), s32[]{:S(2)}) async-start(), calls=%async_computation.16 | async-start | bytes 9799680 | tf_op jit(solution)/shard_map/all_gather | solution.py:66
  9.4 303.3 %all-gather.15.cloned.1.call-start = ((), (), s32[]{:S(2)}) async-start(), calls=%async_computation.15 | async-start | bytes 9799680 | tf_op jit(solution)/shard_map/all_gather | solution.py:66
  10.0 360.1 %all-gather.9.cloned.1.call-start = ((), (), s32[]{:S(2)}) async-start(), calls=%async_computation.12 | async-start | bytes 5898240 | tf_op jit(solution)/shard_map/all_gather | solution.py:339
  82.6 23.4 %copy-start.27 = (f32[512]{0:T(512)}, f32[512]{0:T(512)S(1)}, u32[]{:S(2)}) copy-start(f32[512]{0:T(512)S(1)} %broadcast_multiply_fusion.1) | copy-start | bytes 6148
  83.0 23.1 %copy-start.31 = (f32[512]{0:T(512)}, f32[512]{0:T(512)S(1)}, u32[]{:S(2)}) copy-start(f32[512]{0:T(512)S(1)} %fusion.48) | copy-start | bytes 6148
  84.2 21.8 %copy-start.23 = (f32[1088]{0:T(1024)}, f32[1088]{0:T(1024)S(1)}, u32[]{:S(2)}) copy-start(f32[1088]{0:T(1024)S(1)} %get-tuple-element.41) | copy-start | bytes 13060
  84.2 21.8 %copy-start.41 = (f32[1088]{0:T(1024)}, f32[1088]{0:T(1024)S(1)}, u32[]{:S(2)}) copy-start(f32[1088]{0:T(1024)S(1)} %get-tuple-element.40) | copy-start | bytes 13060
  118.1 311.3 %all-gather.11.cloned.1.call-start = ((), (), s32[]{:S(2)}) async-start(), calls=%async_computation.13 | async-start | bytes 5898240 | tf_op jit(solution)/shard_map/all_gather | solution.py:340
  126.4 516.2 %reduce-scatter.22.cloned.1.call-start = ((), (), s32[]{:S(2)}) async-start(), calls=%async_computation.18 | async-start | bytes 5898240 | tf_op jit(solution)/shard_map/reduce_scatter | solution.py:382
  434.1 18.4 %copy-start.9 = (bf16[1,512,1088]{1,2,0:T(8,128)(2,1)S(1)}, bf16[1,512,1088]{1,2,0:T(8,128)(2,1)}, u32[]{:S(2)}) copy-start(bf16[1,512,1088]{1,2,0:T(8,128)(2,1)} %param.8) | copy-start | bytes 3342340
  434.1 18.4 %copy-start.43 = (f32[1088]{0:T(1024)S(1)}, f32[1088]{0:T(1024)}, u32[]{:S(2)}) copy-start(f32[1088]{0:T(1024)} %get-tuple-element.37) | copy-start | bytes 13060
  457.0 35.5 %copy-start.5 = (f32[512,1088]{0,1:T(8,128)}, f32[512,1088]{0,1:T(8,128)S(1)}, u32[]{:S(2)}) copy-start(f32[512,1088]{0,1:T(8,128)S(1)} %get-tuple-element.43) | copy-start | bytes 6684676
  457.3 35.2 %copy-start.25 = (f32[512]{0:T(512)}, f32[512]{0:T(512)S(1)}, u32[]{:S(2)}) copy-start(f32[512]{0:T(512)S(1)} %fusion.49) | copy-start | bytes 6148
  457.9 9.0 copy-start.11
  457.9 9.0 copy-start.29
  524.2 178.5 %reduce-scatter.20.cloned.1.call-start = ((), (), s32[]{:S(2)}) async-start(), calls=%async_computation.17 | async-start | bytes 5898240 | tf_op jit(solution)/shard_map/reduce_scatter | solution.py:381
  525.0 216.8 %reduce-scatter.26.cloned.1.call-start = ((), (), s32[]{:S(2)}) async-start(), calls=%async_computation.20 | async-start | bytes 2727936 | tf_op jit(solution)/shard_map/reduce_scatter | solution.py:93
  539.2 304.1 %reduce-scatter.28.cloned.1.call-start = ((), (), s32[]{:S(2)}) async-start(), calls=%async_computation.21 | async-start | bytes 10690560 | tf_op jit(solution)/shard_map/reduce_scatter | solution.py:71
  577.8 366.5 %reduce-scatter.30.cloned.1.call-start = ((), (), s32[]{:S(2)}) async-start(), calls=%async_computation.22 | async-start | bytes 10690560 | tf_op jit(solution)/shard_map/reduce_scatter | solution.py:74
  634.4 388.4 %reduce-scatter.24.cloned.1.call-start = ((), (), s32[]{:S(2)}) async-start(), calls=%async_computation.19 | async-start | bytes 8036352 | tf_op jit(solution)/shard_map/reduce_scatter | solution.py:90
  738.3 309.2 %reduce-scatter.36.cloned.1.call-start = ((), (), s32[]{:S(2)}) async-start(), calls=%async_computation.25 | async-start | bytes 378880
  741.7 338.5 %reduce-scatter.32.cloned.1.call-start = ((), (), s32[]{:S(2)}) async-start(), calls=%async_computation.23 | async-start | bytes 73728 | tf_op jit(solution)/shard_map/reduce_scatter | solution.py:96
  751.7 192.6 %copy-start.46 = (u32[32]{0:T(128)S(1)}, u32[32]{0:T(128)}, u32[]{:S(2)}) copy-start(u32[32]{0:T(128)} %constant.99) | copy-start | bytes 388
  752.8 270.0 %copy-start.6 = (f32[512,1088]{0,1:T(8,128)S(1)}, f32[512,1088]{0,1:T(8,128)}, u32[]{:S(2)}) copy-start(f32[512,1088]{0,1:T(8,128)} %copy-done.5) | copy-start | bytes 6684676
  752.8 270.0 %copy-start.40 = (f32[1088]{0:T(1024)S(1)}, f32[1088]{0:T(1024)}, u32[]{:S(2)}) copy-start(f32[1088]{0:T(1024)} %get-tuple-element.35) | copy-start | bytes 13060
  753.6 359.5 %reduce-scatter.38.cloned.1.call-start = ((), (), s32[]{:S(2)}) async-start(), calls=%async_computation.26 | async-start | bytes 1484800
  843.3 304.5 %reduce-scatter.40.cloned.1.call-start = ((), (), s32[]{:S(2)}) async-start(), calls=%async_computation.27 | async-start | bytes 1484800
  944.3 235.5 %reduce-scatter.34.cloned.1.call-start = ((), (), s32[]{:S(2)}) async-start(), calls=%async_computation.24 | async-start | bytes 1116160
  1022.8 26.3 %copy-start.34 = (f32[512]{0:T(512)S(1)}, f32[512]{0:T(512)}, u32[]{:S(2)}) copy-start(f32[512]{0:T(512)} %copy-done.33) | copy-start | bytes 6148
  (35 other events, 103.3 us)
Sparse Core Ops, SparseCore 0:
  10.8 75.6 all-gather.6
  89.4 56.1 all-gather.12
  148.4 80.9 all-gather.16
  232.0 80.6 all-gather.14
  314.4 55.6 all-gather.8
  372.4 57.0 all-gather.10
  524.3 118.2 reduce-scatter.21
  645.6 57.0 reduce-scatter.19
  705.0 36.6 reduce-scatter.25
  744.0 99.2 reduce-scatter.27
  845.7 98.4 reduce-scatter.29
  946.5 76.1 reduce-scatter.23
  1025.6 21.9 reduce-scatter.35
  1050.2 30.0 reduce-scatter.31
  1083.3 29.7 reduce-scatter.37
  1116.2 31.5 reduce-scatter.39
  1151.0 28.6 reduce-scatter.33

commit v2 on v1

--- a/solution.py
+++ b/solution.py
@@ -1,3 +1,6 @@
+import functools
+import math
+
 import jax
 import jax.numpy as jnp
 from jax import lax
@@ -62,55 +65,83 @@
     )
 
 
+def cyclic(size, stride, count, shift):
+    pairs = []
+    for source in range(count):
+        place = (source // stride) % size
+        pairs.append((source, source + (((place + shift) % size) - place) * stride))
+    return pairs
+
+
+def steps_of():
+    depth = lax.axis_size("dp") // 2
+    side = math.isqrt(lax.axis_size("seq"))
+    return {
+        "z": ("dp", depth, 2),
+        "core": ("dp", 2, 1),
+        "outer": ("seq", side, side),
+        "inner": ("seq", side, 1),
+    }
+
+
+def position(step):
+    name, size, stride = step
+    return (lax.axis_index(name) // stride) % size
+
+
+def shifted(values, step, shift):
+    name, size, stride = step
+    return lax.ppermute(values, name, cyclic(size, stride, lax.axis_size(name), shift))
+
+
+def sum_over(values, step, dim):
+    size = step[1]
+    mine = position(step)
+    total = lax.dynamic_index_in_dim(values, mine, dim, keepdims=False).astype(jnp.float32)
+    for shift in range(1, size):
+        piece = lax.dynamic_index_in_dim(values, (mine + shift) % size, dim, keepdims=False)
+        total = total + shifted(piece, step, shift).astype(jnp.float32)
+    return total
+
+
+def collect(values, step, dim):
+    size = step[1]
+    mine = position(step)
+    pieces = [values] + [shifted(values, step, shift) for shift in range(1, size)]
+    return jnp.stack([lax.select_n((mine - at) % size, *pieces) if size > 2 else
+                      jnp.where(mine == at, pieces[0], pieces[1]) for at in range(size)], axis=dim)
+
+
+def scatter_sum(flat, kind=jnp.bfloat16):
+    steps = steps_of()
+    depth, side = steps["z"][1], steps["outer"][1]
+    rows = flat.shape[0] // (2 * depth * side * side)
+    parts = flat.astype(kind).reshape(depth, 2, side, side, rows, flat.shape[1])
+    parts = sum_over(parts, steps["core"], 1).astype(kind)
+    one = sum_over(parts[: depth // 2], steps["inner"], 2).astype(kind)
+    two = sum_over(parts[depth // 2 :], steps["outer"], 1).astype(kind)
+    one = sum_over(one, steps["outer"], 1).astype(kind)
+    two = sum_over(two, steps["inner"], 1).astype(kind)
+    return sum_over(jnp.concatenate([one, two], axis=0), steps["z"], 0)
+
+
+def gather_all(flat):
+    steps = steps_of()
+    depth, side = steps["z"][1], steps["outer"][1]
+    lines = collect(flat, steps["z"], 0)
+    one = collect(lines[: depth // 2], steps["outer"], 1)
+    two = collect(lines[depth // 2 :], steps["inner"], 1)
+    one = collect(one, steps["inner"], 2)
+    two = collect(two, steps["outer"], 1)
+    parts = jnp.concatenate([one, two], axis=0)
+    return collect(parts, steps["core"], 1).reshape(-1, flat.shape[1])
+
+
 def fetch(*flat_weights):
-    return tuple(lax.all_gather(flat, ("dp", "seq"), axis=0, tiled=True) for flat in flat_weights)
-
-
-def reduce_mlp(grad_up_flat, grad_down_flat):
-    by_row = (
-        lax.psum_scatter(
-            grad_up_flat.astype(jnp.bfloat16), "dp", scatter_dimension=0, tiled=True
-        ).astype(jnp.float32),
-        lax.psum_scatter(
-            grad_down_flat.astype(jnp.bfloat16), "dp", scatter_dimension=0, tiled=True
-        ).astype(jnp.float32),
-    )
-    return (
-        lax.psum_scatter(
-            by_row[0].astype(jnp.bfloat16), "seq", scatter_dimension=0, tiled=True
-        ).astype(jnp.float32),
-        lax.psum_scatter(
-            by_row[1].astype(jnp.bfloat16), "seq", scatter_dimension=0, tiled=True
-        ).astype(jnp.float32),
-    )
-
-
-def reduce_attention(grad_qkv_flat, grad_out_flat, grad_vec_flat):
-    by_row = (
-        lax.psum_scatter(
-            grad_qkv_flat.astype(jnp.bfloat16), "dp", scatter_dimension=0, tiled=True
-        ).astype(jnp.float32),
-        lax.psum_scatter(
-            grad_out_flat.astype(jnp.bfloat16), "dp", scatter_dimension=0, tiled=True
-        ).astype(jnp.float32),
-        lax.psum_scatter(
-            grad_vec_flat.astype(jnp.bfloat16), "dp", scatter_dimension=0, tiled=True
-        ).astype(jnp.float32),
-    )
-    return (
-        lax.psum_scatter(
-            by_row[0].astype(jnp.bfloat16), "seq", scatter_dimension=0, tiled=True
-        ).astype(jnp.float32),
-        lax.psum_scatter(
-            by_row[1].astype(jnp.bfloat16), "seq", scatter_dimension=0, tiled=True
-        ).astype(jnp.float32),
-        lax.psum_scatter(
-            by_row[2].astype(jnp.bfloat16), "seq", scatter_dimension=0, tiled=True
-        ).astype(jnp.float32),
-    )
-
-
-KEY_TILE = 256
+    return tuple(gather_all(flat) for flat in flat_weights)
+
+
+SEGMENT_MOST = 1024
 LANES = 128
 
 
@@ -142,7 +173,7 @@
 
 
 def forward_kernel(
-    bounds_ref, q_ref, k_ref, v_ref, starts_ref, places_ref, o_ref, lse_ref, top, total, acc
+    tile_rows, bounds_ref, q_ref, k_ref, v_ref, starts_ref, places_ref, o_ref, lse_ref, top, total, acc
 ):
     rows = q_ref.shape[0]
     stacked = stack_pair(q_ref[...])
@@ -153,9 +184,9 @@
     acc[...] = jnp.zeros_like(acc)
 
     def step(tile, carry):
-        offset = pl.multiple_of(tile * KEY_TILE, KEY_TILE)
-        keys = k_ref[pl.ds(offset, KEY_TILE), :]
-        values = v_ref[pl.ds(offset, KEY_TILE), :]
+        offset = pl.multiple_of(tile * tile_rows, tile_rows)
+        keys = k_ref[pl.ds(offset, tile_rows), :]
+        values = v_ref[pl.ds(offset, tile_rows), :]
         scores = masked_scores(bounds_ref, keys, stacked, starts, places, offset)
         old_top = top[...]
         new_top = jnp.maximum(old_top, jnp.max(scores, axis=0, keepdims=True))
@@ -172,7 +203,7 @@
 
 
 def backward_kernel(
-    bounds_ref, q_ref, k_ref, v_ref, g_ref, o_ref, lse_ref, starts_ref, places_ref,
+    tile_rows, bounds_ref, q_ref, k_ref, v_ref, g_ref, o_ref, lse_ref, starts_ref, places_ref,
     dq_ref, dk_ref, dv_ref, acc,
 ):
     rows = q_ref.shape[0]
@@ -196,17 +227,17 @@
     dv_ref[...] = jnp.zeros_like(dv_ref)
 
     def step(tile, carry):
-        offset = pl.multiple_of(tile * KEY_TILE, KEY_TILE)
-        keys = k_ref[pl.ds(offset, KEY_TILE), :]
-        values = v_ref[pl.ds(offset, KEY_TILE), :]
+        offset = pl.multiple_of(tile * tile_rows, tile_rows)
+        keys = k_ref[pl.ds(offset, tile_rows), :]
+        values = v_ref[pl.ds(offset, tile_rows), :]
         scores = masked_scores(bounds_ref, keys, stacked, starts, places, offset)
         probs = jnp.exp(scores - totals)
         d_probs = contract(values, stacked_g, 1, 1)
         d_scores = (probs * (d_probs - row_dots)).astype(jnp.bfloat16)
-        dv_ref[pl.ds(offset, KEY_TILE), :] = contract(
+        dv_ref[pl.ds(offset, tile_rows), :] = contract(
             probs.astype(jnp.bfloat16), stacked_g, 1, 0
         ).astype(dv_ref.dtype)
-        dk_ref[pl.ds(offset, KEY_TILE), :] = contract(d_scores, stacked, 1, 0).astype(dk_ref.dtype)
+        dk_ref[pl.ds(offset, tile_rows), :] = contract(d_scores, stacked, 1, 0).astype(dk_ref.dtype)
         acc[...] += contract(keys, d_scores, 0, 0)
         return carry
 
@@ -214,8 +245,8 @@
     dq_ref[...] = unstack_pair(acc[...], rows).T
 
 
-def column_spec(rows):
-    return pl.BlockSpec((rows, LANES), lambda pair, bounds: (0, pair))
+def column_spec(rows, first=0):
+    return pl.BlockSpec((rows, LANES), lambda pair, bounds: (0, first + pair))
 
 
 def whole_spec(cols):
@@ -226,17 +257,17 @@
     return pl.BlockSpec((1, 1, cols), lambda pair, bounds: (pair, 0, 0))
 
 
-def attend(bounds, queries, keys, values, starts, places):
+def attend(tile_rows, bounds, queries, keys_values, starts, places):
     rows, width = queries.shape
-    length = keys.shape[0]
+    length = keys_values.shape[0]
     pairs = width // LANES
     return pl.pallas_call(
-        forward_kernel,
+        functools.partial(forward_kernel, tile_rows),
         grid_spec=pltpu.PrefetchScalarGridSpec(
             num_scalar_prefetch=1,
             grid=(pairs,),
             in_specs=[
-                column_spec(rows), column_spec(length), column_spec(length),
+                column_spec(rows), column_spec(length), column_spec(length, pairs),
                 whole_spec(2 * rows), whole_spec(2 * rows),
             ],
             out_specs=[column_spec(rows), pair_spec(2 * rows)],
@@ -256,20 +287,20 @@
             transcendentals=rows * length * width // 64,
         ),
         name="attention_forward",
-    )(bounds, queries, keys, values, starts, places)
-
-
-def attend_back(bounds, queries, keys, values, grads, mixed, totals, starts, places):
+    )(bounds, queries, keys_values, keys_values, starts, places)
+
+
+def attend_back(tile_rows, bounds, queries, keys_values, grads, mixed, totals, starts, places):
     rows, width = queries.shape
-    length = keys.shape[0]
+    length = keys_values.shape[0]
     pairs = width // LANES
     return pl.pallas_call(
-        backward_kernel,
+        functools.partial(backward_kernel, tile_rows),
         grid_spec=pltpu.PrefetchScalarGridSpec(
             num_scalar_prefetch=1,
             grid=(pairs,),
             in_specs=[
-                column_spec(rows), column_spec(length), column_spec(length),
+                column_spec(rows), column_spec(length), column_spec(length, pairs),
                 column_spec(rows), column_spec(rows), pair_spec(2 * rows),
                 whole_spec(2 * rows), whole_spec(2 * rows),
             ],
@@ -287,7 +318,7 @@
             transcendentals=rows * length * width // 64,
         ),
         name="attention_backward",
-    )(bounds, queries, keys, values, grads, mixed, totals, starts, places)
+    )(bounds, queries, keys_values, keys_values, grads, mixed, totals, starts, places)
 
 
 def body(hidden_in, segments, cotangent, w_qkv, w_out, w_up, w_down, vectors):
@@ -330,15 +361,26 @@
     queries = widen(queries * jnp.bfloat16(score_scale))
     key_rows = widen(key_rows)
     value_rows = widen(value_rows)
+    ranks = lax.axis_size("seq")
+    behind = min(ranks - 1, pl.cdiv(SEGMENT_MOST - 1, tok_rows))
+    tile_rows = math.gcd(tok_rows, 256)
+    window_first = query_first - behind * tok_rows
     query_starts = jnp.sum(
         (seg_row[None, :] < query_segs[:, None]).astype(jnp.int32), axis=1, dtype=jnp.int32
     )
-    bounds = jnp.stack([query_starts[0] // KEY_TILE, pl.cdiv(query_first + tok_rows, KEY_TILE)])
+    query_starts = query_starts - window_first
+    bounds = jnp.stack(
+        [query_starts[0] // tile_rows, jnp.int32((behind + 1) * tok_rows // tile_rows)]
+    )
     starts = jnp.tile(query_starts, 2)[None]
-    places = jnp.tile(query_places, 2)[None]
-    key_all = lax.all_gather(key_rows, "seq", axis=0, tiled=True)
-    value_all = lax.all_gather(value_rows, "seq", axis=0, tiled=True)
-    attended_f, log_total = attend(bounds, queries, key_all, value_all, starts, places)
+    places = jnp.tile(query_places - window_first, 2)[None]
+    own_pair = jnp.concatenate([key_rows, value_rows], axis=1)
+    window = [own_pair]
+    for back in range(1, behind + 1):
+        pairs = [(rank, rank + back) for rank in range(ranks - back)]
+        window.insert(0, lax.ppermute(own_pair, "seq", pairs))
+    keys_values = jnp.concatenate(window, axis=0)
+    attended_f, log_total = attend(tile_rows, bounds, queries, keys_values, starts, places)
     attended = attended_f[:, :model_width].astype(jnp.bfloat16)
     middle = (
         tokens + jnp.dot(attended, fwd_weights[1], preferred_element_type=jnp.float32) + bias_proj
@@ -364,10 +406,8 @@
     d_normed_two = jnp.dot(d_before, back_weights[2].T, preferred_element_type=jnp.float32)
     d_middle_norm, d_gain_two, d_shift_two = pull_two(d_normed_two)
     d_middle = cot_float + d_middle_norm
-    mlp_grads = reduce_mlp(
-        to_flat(grad_up_full, w_up.shape[0] * spread_count),
-        to_flat(grad_down_full, w_down.shape[0] * spread_count),
-    )
+    grad_down = scatter_sum(to_flat(grad_down_full, w_down.shape[0] * spread_count))
+    grad_up = scatter_sum(to_flat(grad_up_full, w_up.shape[0] * spread_count))
     d_proj = d_middle.astype(jnp.bfloat16)
     d_bias_proj = jnp.sum(d_middle, axis=0)
     grad_out_full = jnp.dot(attended.T, d_proj, preferred_element_type=jnp.float32)
@@ -375,11 +415,20 @@
         jnp.bfloat16
     )
     dq_sum, key_terms, value_terms = attend_back(
-        bounds, queries, key_all, value_all, widen(d_attended), attended_f, log_total, starts,
+        tile_rows, bounds, queries, keys_values, widen(d_attended), attended_f, log_total, starts,
         places,
     )
-    d_key = lax.psum_scatter(key_terms, "seq", scatter_dimension=0, tiled=True)[:, :model_width]
-    d_value = lax.psum_scatter(value_terms, "seq", scatter_dimension=0, tiled=True)[:, :model_width]
+
+    def to_owner(terms):
+        total = terms[behind * tok_rows :].astype(jnp.float32)
+        for back in range(1, behind + 1):
+            piece = terms[(behind - back) * tok_rows : (behind - back + 1) * tok_rows]
+            pairs = [(rank, rank - back) for rank in range(back, ranks)]
+            total = total + lax.ppermute(piece, "seq", pairs).astype(jnp.float32)
+        return total[:, :model_width].astype(jnp.bfloat16)
+
+    d_key = to_owner(key_terms)
+    d_value = to_owner(value_terms)
     d_query = (score_scale * dq_sum[:, :model_width]).astype(jnp.bfloat16)
     d_packed = jnp.concatenate([d_query, d_key, d_value], axis=1)
     grad_qkv_full = jnp.dot(normed.T, d_packed, preferred_element_type=jnp.float32)
@@ -399,20 +448,12 @@
             d_bias_down,
         ]
     )
-    attn_grads = reduce_attention(
-        to_flat(grad_qkv_full, w_qkv.shape[0] * spread_count),
-        to_flat(grad_out_full, w_out.shape[0] * spread_count),
-        to_flat(vector_grads, vectors.shape[0] * spread_count),
-    )
-    return (
-        hidden_out,
-        grad_in,
-        attn_grads[0],
-        attn_grads[1],
-        mlp_grads[0],
-        mlp_grads[1],
-        attn_grads[2],
-    )
+    grad_out = scatter_sum(to_flat(grad_out_full, w_out.shape[0] * spread_count))
+    grad_qkv = scatter_sum(to_flat(grad_qkv_full, w_qkv.shape[0] * spread_count))
+    grad_vec = scatter_sum(
+        to_flat(vector_grads, vectors.shape[0] * spread_count), jnp.float32
+    )
+    return (hidden_out, grad_in, grad_qkv, grad_out, grad_up, grad_down, grad_vec)
 
 
 def solution(mesh):

time: 1200 us -> 924 us (0.77)
  waiting for transfers between devices: 698 us -> 233 us
  starting transfers between devices: 1.24 us -> 180 us
  other arithmetic: 21.5 us -> 123 us
  blocking collectives: 81.3 us -> 0 us
  between operations: 18.1 us -> 5.71 us
    reduce_scatter x7 -> x0, waiting for transfers between devices: 361 us -> none  [the longest x1 101 us: reduce_mlp(): lax.psum_scatter(grad_down_flat.astype(jnp.bfloat16), 'dp', scatter_dimen...]
    all_gather x6 -> x0, waiting for transfers between devices: 237 us -> none  [the longest x4 147 us: fetch(): lax.all_gather(flat, ('dp', 'seq'), axis=0, tiled=True)]
    ppermute x0 -> x86, waiting for transfers between devices: none -> 233 us  [the longest x80 233 us: shifted(): lax.ppermute(values, name, cyclic(size, stride, lax.axis_size(name), shift))]
    ppermute x0 -> x86, starting transfers between devices: none -> 180 us  [the longest x80 167 us: shifted(): lax.ppermute(values, name, cyclic(size, stride, lax.axis_size(name), shift))]
    unnamed x21 -> x0, waiting for transfers between devices: 100 us -> none
    all_gather x1 -> x0, blocking collectives: 71.1 us -> none  [fetch(): lax.all_gather(flat, ('dp', 'seq'), axis=0, tiled=True)]
    another operation x1 -> x57, other arithmetic: 0.08 us -> 58.2 us  [the longest x55 55.1 us: collect(): jnp.stack([lax.select_n((mine - at) % size, *pieces) if size > 2 else jnp...]
    convert_element_type x5 -> x0, local copies, waits for them, and re-layouts: 28.4 us -> none  [the longest x1 9.33 us: reduce_mlp(): grad_down_flat.astype(jnp.bfloat16)]
  transfers between devices with their start and end apart: 17 -> 86, of which waited for: 17 -> 37; matrix products, arithmetic and copies ran while one was open for 24% -> 39% of each run, Pallas kernels for 0% -> 0%
where the time goes in v2:
time: 924 us; the launch traced here: 910 us
  waiting for transfers between devices  233 us (25%)
  local copies, waits for them, and re-layouts  227 us (25%)
  starting transfers between devices  180 us (19%)
  other arithmetic  123 us (13%)
  matrix products  98.5 us (11%)
  Pallas kernels  42.4 us (5%)
    ppermute x80, waiting for transfers between devices, shifted(): lax.ppermute(values, name, cyclic(size, stride, lax.axis_size(name), shift))  233 us
    ppermute x80, starting transfers between devices, shifted(): lax.ppermute(values, name, cyclic(size, stride, lax.axis_size(name), shift))  167 us
    reshape x4, local copies, waits for them, and re-layouts, to_flat(): flat_values = grad_matrix.reshape(-1)  57.8 us
    another operation x55, other arithmetic, collect(): jnp.stack([lax.select_n((mine - at) % size, *pieces) if size > 2 else jnp...  55.1 us
    reshape x4, local copies, waits for them, and re-layouts, take_matrix(): flat_rows.reshape(-1)[:row_count * col_count].reshape(row_count, col_count)  51.2 us
    unnamed x209, local copies, waits for them, and re-layouts  24.8 us
    pallas_call x1, Pallas kernels, attend_back(): pl.pallas_call(functools.partial(backward_kernel, tile_rows), grid_spec=p...  24.5 us
    slice x4, local copies, waits for them, and re-layouts, take_matrix(): flat_rows.reshape(-1)[:row_count * col_count].reshape(row_count, col_count)  21.8 us
  transfers between devices with their start and end apart: 86, of which 37 were waited for; matrix products, arithmetic and copies ran while one was open for 39% of the time, Pallas kernels for 0%

profile of v2, /device:TPU:0, one launch (start us, length us, event | category | flops | bytes accessed | tf_op | source)
XLA Modules:
  0.0 910.1 jit_solution(18257594770336681210)
XLA Ops:
  47.9 8.7 collective-permute-start.27
  79.7 15.5 %collective-permute-done.27 = bf16[1160,128]{1,0:T(8,128)(2,1)S(1)} collective-permute-done((bf16[1160,128]{1,0:T(8,128)(2,1)S(1)}, bf16[1160,128]{1,0:T(8,128)(2,1)S(1)}, u32[]{:S(2)}, u32[]{:S(2)}) %collective-permute-start.27) | collective-permute-done | bytes 296992 | tf_op jit(solution)/shard_map/ppermute | solution.py:94
  109.5 10.1 %collective-permute-done.39 = bf16[2,1160,128]{2,1,0:T(8,128)(2,1)S(1)} collective-permute-done((bf16[2,1160,128]{2,1,0:T(8,128)(2,1)S(1)}, bf16[2,1160,128]{2,1,0:T(8,128)(2,1)S(1)}, u32[]{:S(2)}, u32[]{:S(2)}) %collective-permute-start.39) | collective-permute-done | bytes 593952 | tf_op jit(solution)/shard_map/ppermute | solution.py:94
  137.0 14.0 %collective-permute-done.14 = bf16[2,2,872,128]{3,2,1,0:T(8,128)(2,1)S(1)} collective-permute-done((bf16[2,2,872,128]{3,2,1,0:T(8,128)(2,1)S(1)}, bf16[2,2,872,128]{3,2,1,0:T(8,128)(2,1)S(1)}, u32[]{:S(2)}, u32[]{:S(2)}) %collective-permute-start.14) | collective-permute-done | bytes 892960 | tf_op jit(solution)/shard_map/ppermute | solution.py:94
  161.2 15.4 %collective-permute-done.40 = bf16[2,2,1160,128]{3,2,0,1:T(8,128)(2,1)} collective-permute-done((bf16[2,2,1160,128]{3,2,0,1:T(8,128)(2,1)}, bf16[2,2,1160,128]{3,2,0,1:T(8,128)(2,1)}, u32[]{:S(2)}, u32[]{:S(2)}) %collective-permute-start.40) | collective-permute-done | bytes 1187872 | tf_op jit(solution)/shard_map/ppermute | solution.py:94
  183.7 15.0 %collective-permute-done.32 = bf16[2,2,1160,128]{3,2,1,0:T(8,128)(2,1)} collective-permute-done((bf16[2,2,1160,128]{3,2,1,0:T(8,128)(2,1)}, bf16[2,2,1160,128]{3,2,1,0:T(8,128)(2,1)}, u32[]{:S(2)}, u32[]{:S(2)}) %collective-permute-start.32) | collective-permute-done | bytes 1187872 | tf_op jit(solution)/shard_map/ppermute | solution.py:94
  216.8 13.1 %reshape.216 = bf16[1088,3264]{1,0:T(8,128)(2,1)} reshape(bf16[3551232]{0:T(1024)(128)(2,1)} %slice.174) | data formatting | bytes 14204928 | tf_op jit(solution)/shard_map/reshape | solution.py:50
  285.7 9.1 %slice.187 = bf16[4734976]{0:T(1024)(128)(2,1)} slice(bf16[4751360]{0:T(1024)(128)(2,1)} %bitcast.486), slice={[0:4734976]} | slice | bytes 18939904 | tf_op jit(solution)/shard_map/slice | solution.py:50
  294.9 17.0 %reshape.219 = bf16[4352,1088]{1,0:T(8,128)(2,1)} reshape(bf16[4734976]{0:T(1024)(128)(2,1)} %slice.187) | data formatting | bytes 18939904 | tf_op jit(solution)/shard_map/reshape | solution.py:50
  311.9 9.0 select_bitcast_fusion.3
  320.9 8.3 pad_maximum_fusion
  329.2 9.1 %slice.185 = bf16[4734976]{0:T(1024)(128)(2,1)} slice(bf16[4751360]{0:T(1024)(128)(2,1)} %bitcast.485), slice={[0:4734976]} | slice | bytes 18939904 | tf_op jit(solution)/shard_map/slice | solution.py:50
  338.3 17.8 %reshape.218 = bf16[1088,4352]{1,0:T(8,128)(2,1)} reshape(bf16[4734976]{0:T(1024)(128)(2,1)} %slice.185) | data formatting | bytes 18939904 | tf_op jit(solution)/shard_map/reshape | solution.py:50
  362.3 17.9 %attention_forward.1 = (f32[512,1152]{1,0:T(8,128)S(1)}, f32[9,1,1024]{2,1,0:T(1,128)S(1)}) custom-call(s32[2]{0:T(128)S(1)} %pad_add_fusion.bounds_ref, bf16[512,1152]{1,0:T(8,128)(2,1)S(1)} %pad.36.q_ref, bf16[1536,2304]{1,0:T(8,128)(2,1)S(1)} %maximum_maximum_fusion.k_ref.v_ref, bf16[1536,2304]{1,0:T(8,128)(2,1)S(1)} %maximum_maximum_fusion.k_ref.v_ref, ...), custom_call_target="tpu_custom_call" | custom-call | flops 7247757312 | bytes 14155776 | tf_op jit(solution)/shard_map/attention_forward/pallas_call | solution.py:264
  386.1 8.7 fusion.133
  394.9 18.0 %convert_reduce_fusion = (f32[4352]{0:T(1024)}, bf16[512,4352]{1,0:T(8,128)(2,1)}) fusion(f32[512,4352]{1,0:T(8,128)} %fusion.133, f32[4352]{0:T(1024)S(1)} %copy-done.70, bf16[4352,1088]{1,0:T(8,128)(2,1)} %reshape.219, bf16[1,512,1088]{1,2,0:T(8,128)(2,1)S(1)} %copy-done.55), kind=kOutput, calls=%fused_computation.23 | convolution fusion | flops 4899860480 | bytes 23988224 | tf_op jit(solution)/shard_map/dot_general | solution.py:402
  412.9 10.0 %multiply_reduce_fusion = (f32[1088]{0:T(1024)}, f32[512]{0:T(512)S(1)}, f32[1088]{0:T(1024)}, f32[512,1088]{0,1:T(8,128)S(1)}) fusion(f32[512,1088]{0,1:T(8,128)} %copy-done.7, f32[512]{0:T(512)S(1)} %fusion.132, f32[512]{0:T(512)S(1)} %broadcast_multiply_fusion, f32[1088]{0:T(1024)S(1)} %copy-done.63, bf16[512,4352]{1,0:T(8,128)(2,1)} %get-tuple-element.157, ...), kind=kOutput, calls=%fused_computation.95 | convolution fusion | flops 4853069312 | bytes 18402048 | tf_op jit(solution)/shard_map/dot_general | solution.py:406
  450.3 24.5 %attention_backward.1 = (f32[512,1152]{1,0:T(8,128)S(1)}, bf16[1536,1152]{1,0:T(8,128)(2,1)}, bf16[1536,1152]{1,0:T(8,128)(2,1)}) custom-call(s32[2]{0:T(128)S(1)} %pad_add_fusion.bounds_ref, bf16[512,1152]{1,0:T(8,128)(2,1)S(1)} %pad.36.q_ref, bf16[1536,2304]{1,0:T(8,128)(2,1)} %copy-done, bf16[1536,2304]{1,0:T(8,128)(2,1)} %copy-done, ...), custom_call_target="tpu_custom_call" | custom-call | flops 18119393280 | bytes 21233664 | tf_op jit(solution)/shard_map/attention_backward/pallas_call | solution.py:297
  496.3 18.3 %reshape.222 = bf16[4734976]{0:T(1024)(128)(2,1)} reshape(bf16[1088,4352]{1,0:T(8,128)(2,1)} %convolution_convert_fusion.1) | data formatting | bytes 18939904 | tf_op jit(solution)/shard_map/reshape | solution.py:54
  526.2 13.9 %copy.179 = bf16[4352,1088]{1,0:T(8,128)(2,1)} copy(bf16[4352,1088]{0,1:T(8,128)(2,1)} %convolution_convert_fusion) | data formatting | bytes 18939904 | tf_op jit(solution)/shard_map/convert.27
  540.1 19.4 %reshape.223 = bf16[4734976]{0:T(1024)(128)(2,1)} reshape(bf16[4352,1088]{1,0:T(8,128)(2,1)} %copy.179) | data formatting | bytes 18939904 | tf_op jit(solution)/shard_map/reshape | solution.py:54
  584.2 9.1 fusion.134
  599.6 13.9 %reshape.220 = bf16[3551232]{0:T(1024)(128)(2,1)} reshape(bf16[1088,3264]{1,0:T(8,128)(2,1)} %convolution_convert_fusion.2) | data formatting | bytes 14204928 | tf_op jit(solution)/shard_map/reshape | solution.py:54
  631.8 27.9 %collective-permute-start.55 = (bf16[2,2,296,128]{3,2,0,1:T(8,128)(2,1)S(1)}, bf16[2,2,296,128]{3,2,0,1:T(8,128)(2,1)S(1)}, u32[]{:S(2)}, u32[]{:S(2)}) collective-permute-start(bf16[2,2,296,128]{3,2,0,1:T(8,128)(2,1)S(1)} %bitcast.500), channel_id=1, source_target_pairs={{0,1},{1,0},{2,3},{3,2},{4,5},{5,4},{6,7},{7,6},{8,9},{9,8},{10,11... | collective-permute-start | bytes 909320 | tf_op jit(solution)/shard_map/ppermute | solution.py:94
  682.9 34.8 %collective-permute-start.85 = (f32[8,128]{1,0:T(8,128)S(1)}, f32[8,128]{1,0:T(8,128)S(1)}, u32[]{:S(2)}, u32[]{:S(2)}) collective-permute-start(f32[8,128]{1,0:T(8,128)S(1)} %get-tuple-element.139), channel_id=1, source_target_pairs={{0,24},{4,28},{8,0},{12,4},{16,8},{20,12},{24,16},{28,20},{1,25},{... | collective-permute-start | bytes 12296 | tf_op jit(solution)/shard_map/ppermute | solution.py:94
  738.9 13.0 %fusion.21 = bf16[1,512,1088]{1,2,0:T(8,128)(2,1)} fusion(f32[512,1088]{0,1:T(8,128)S(1)} %copy-done.9, bf16[4352,1088]{1,0:T(8,128)(2,1)} %reshape.219, f32[1088]{0:T(1024)S(1)} %copy-done.80, f32[512,4352]{1,0:T(8,128)} %fusion.133, f32[4352]{0:T(1024)S(1)} %copy-done.71), kind=kOutput, calls=%fused_computation.61 | convolution fusion | flops 4872568832 | bytes 21746944 | tf_op jit(solution)/shard_map/dot_general | solution.py:394
  794.1 19.2 %collective-permute-done.63 = bf16[2,2,1160,128]{3,2,0,1:T(8,128)(2,1)} collective-permute-done((bf16[2,2,1160,128]{3,2,0,1:T(8,128)(2,1)}, bf16[2,2,1160,128]{3,2,0,1:T(8,128)(2,1)}, u32[]{:S(2)}, u32[]{:S(2)}) %collective-permute-start.63) | collective-permute-done | bytes 1187872 | tf_op jit(solution)/shard_map/ppermute | solution.py:94
  820.5 18.2 %collective-permute-done.71 = bf16[2,2,1160,128]{3,2,0,1:T(8,128)(2,1)S(1)} collective-permute-done((bf16[2,2,1160,128]{3,2,0,1:T(8,128)(2,1)S(1)}, bf16[2,2,1160,128]{3,2,0,1:T(8,128)(2,1)S(1)}, u32[]{:S(2)}, u32[]{:S(2)}) %collective-permute-start.71) | collective-permute-done | bytes 1187872 | tf_op jit(solution)/shard_map/ppermute | solution.py:94
  841.8 9.2 %collective-permute-done.48 = bf16[2,872,128]{2,1,0:T(8,128)(2,1)S(1)} collective-permute-done((bf16[2,872,128]{2,1,0:T(8,128)(2,1)S(1)}, bf16[2,872,128]{2,1,0:T(8,128)(2,1)S(1)}, u32[]{:S(2)}, u32[]{:S(2)}) %collective-permute-start.48) | collective-permute-done | bytes 446496 | tf_op jit(solution)/shard_map/ppermute | solution.py:94
  854.8 8.9 collective-permute-done.53
  864.2 14.9 %collective-permute-done.52 = bf16[872,128]{1,0:T(8,128)(2,1)S(1)} collective-permute-done((bf16[872,128]{1,0:T(8,128)(2,1)S(1)}, bf16[872,128]{1,0:T(8,128)(2,1)S(1)}, u32[]{:S(2)}, u32[]{:S(2)}) %collective-permute-start.52) | collective-permute-done | bytes 223264 | tf_op jit(solution)/shard_map/ppermute | solution.py:94
  899.0 9.6 %collective-permute-done.76 = bf16[1160,128]{1,0:T(8,128)(2,1)S(1)} collective-permute-done((bf16[1160,128]{1,0:T(8,128)(2,1)S(1)}, bf16[1160,128]{1,0:T(8,128)(2,1)S(1)}, u32[]{:S(2)}, u32[]{:S(2)}) %collective-permute-start.76) | collective-permute-done | bytes 296992 | tf_op jit(solution)/shard_map/ppermute | solution.py:94
  (552 shorter events, 433.0 us)
Async XLA Ops:
  39.5 36.6 %collective-permute-start.35 = (bf16[1160,128]{1,0:T(8,128)(2,1)S(1)}, bf16[1160,128]{1,0:T(8,128)(2,1)S(1)}, u32[]{:S(2)}, u32[]{:S(2)}) collective-permute-start(bf16[1160,128]{1,0:T(8,128)(2,1)S(1)} %copy-done.60), channel_id=1, source_target_pairs={{0,16},{4,20},{8,24},{12,28},{16,0},{20,4},{24,8},{28,12},{1,17},{... | collective-permute-start | bytes 890888 | tf_op jit(solution)/shard_map/ppermute | solution.py:94
  41.1 35.0 %collective-permute-start.36 = (bf16[1160,128]{1,0:T(8,128)(2,1)S(1)}, bf16[1160,128]{1,0:T(8,128)(2,1)S(1)}, u32[]{:S(2)}, u32[]{:S(2)}) collective-permute-start(bf16[1160,128]{1,0:T(8,128)(2,1)S(1)} %copy-done.60), channel_id=1, source_target_pairs={{0,24},{4,28},{8,0},{12,4},{16,8},{20,12},{24,16},{28,20},{1,25},{... | collective-permute-start | bytes 890888 | tf_op jit(solution)/shard_map/ppermute | solution.py:94
  47.9 47.3 %collective-permute-start.27 = (bf16[1160,128]{1,0:T(8,128)(2,1)S(1)}, bf16[1160,128]{1,0:T(8,128)(2,1)S(1)}, u32[]{:S(2)}, u32[]{:S(2)}) collective-permute-start(bf16[1160,128]{1,0:T(8,128)(2,1)S(1)} %copy-done.61), channel_id=1, source_target_pairs={{0,16},{4,20},{8,24},{12,28},{16,0},{20,4},{24,8},{28,12},{1,17},{... | collective-permute-start | bytes 890888 | tf_op jit(solution)/shard_map/ppermute | solution.py:94
  109.3 47.7 %collective-permute-start.25 = (bf16[4,2,2,296,128]{4,3,2,1,0:T(8,128)(2,1)S(1)}, bf16[4,2,2,296,128]{4,3,2,1,0:T(8,128)(2,1)S(1)}, u32[]{:S(2)}, u32[]{:S(2)}) collective-permute-start(bf16[4,2,2,296,128]{4,3,2,1,0:T(8,128)(2,1)S(1)} %maximum_maximum_fusion.4), channel_id=1, source_target_pairs={{0,4},{4,0},{8,12},{12,8},{16,20},{20,16},{24,28},{28,24},{1,5},{5... | collective-permute-start | bytes 3637256 | tf_op jit(solution)/shard_map/ppermute | solution.py:94
  132.3 44.3 %collective-permute-start.40 = (bf16[2,2,1160,128]{3,2,0,1:T(8,128)(2,1)}, bf16[2,2,1160,128]{3,2,0,1:T(8,128)(2,1)}, u32[]{:S(2)}, u32[]{:S(2)}) collective-permute-start(bf16[2,2,1160,128]{3,2,0,1:T(8,128)(2,1)} %pad_maximum_fusion.10), channel_id=1, source_target_pairs={{0,2},{1,3},{2,0},{3,1},{4,6},{5,7},{6,4},{7,5},{8,10},{9,11},{10,... | collective-permute-start | bytes 3563528 | tf_op jit(solution)/shard_map/ppermute | solution.py:94
  132.9 45.5 %collective-permute-start.38 = (bf16[2,2,1160,128]{3,2,0,1:T(8,128)(2,1)}, bf16[2,2,1160,128]{3,2,0,1:T(8,128)(2,1)}, u32[]{:S(2)}, u32[]{:S(2)}) collective-permute-start(bf16[2,2,1160,128]{3,2,0,1:T(8,128)(2,1)} %pad_maximum_fusion.9), channel_id=1, source_target_pairs={{0,1},{1,0},{2,3},{3,2},{4,5},{5,4},{6,7},{7,6},{8,9},{9,8},{10,11... | collective-permute-start | bytes 3563528 | tf_op jit(solution)/shard_map/ppermute | solution.py:94
  151.1 47.6 %collective-permute-start.32 = (bf16[2,2,1160,128]{3,2,1,0:T(8,128)(2,1)}, bf16[2,2,1160,128]{3,2,1,0:T(8,128)(2,1)}, u32[]{:S(2)}, u32[]{:S(2)}) collective-permute-start(bf16[2,2,1160,128]{3,2,1,0:T(8,128)(2,1)} %pad_maximum_fusion.8), channel_id=1, source_target_pairs={{0,2},{1,3},{2,0},{3,1},{4,6},{5,7},{6,4},{7,5},{8,10},{9,11},{10,... | collective-permute-start | bytes 3563528 | tf_op jit(solution)/shard_map/ppermute | solution.py:94
  152.8 47.4 %collective-permute-start.30 = (bf16[2,2,1160,128]{3,2,0,1:T(8,128)(2,1)}, bf16[2,2,1160,128]{3,2,0,1:T(8,128)(2,1)}, u32[]{:S(2)}, u32[]{:S(2)}) collective-permute-start(bf16[2,2,1160,128]{3,2,0,1:T(8,128)(2,1)} %pad_maximum_fusion.7), channel_id=1, source_target_pairs={{0,1},{1,0},{2,3},{3,2},{4,5},{5,4},{6,7},{7,6},{8,9},{9,8},{10,11... | collective-permute-start | bytes 3563528 | tf_op jit(solution)/shard_map/ppermute | solution.py:94
  157.0 48.8 %collective-permute-start.15 = (bf16[4,2,2,872,128]{4,3,2,1,0:T(8,128)(2,1)}, bf16[4,2,2,872,128]{4,3,2,1,0:T(8,128)(2,1)}, u32[]{:S(2)}, u32[]{:S(2)}) collective-permute-start(bf16[4,2,2,872,128]{4,3,2,1,0:T(8,128)(2,1)} %maximum_maximum_fusion.3), channel_id=1, source_target_pairs={{0,4},{4,0},{8,12},{12,8},{16,20},{20,16},{24,28},{28,24},{1,5},{5... | collective-permute-start | bytes 10715144 | tf_op jit(solution)/shard_map/ppermute | solution.py:94
  183.7 78.6 %collective-permute-start.41 = (bf16[4,2,2,1160,128]{4,3,0,2,1:T(8,128)(2,1)}, bf16[4,2,2,1160,128]{4,3,0,2,1:T(8,128)(2,1)}, u32[]{:S(2)}, u32[]{:S(2)}) collective-permute-start(bf16[4,2,2,1160,128]{4,3,0,2,1:T(8,128)(2,1)} %maximum_maximum_fusion.2), channel_id=1, source_target_pairs={{0,4},{4,0},{8,12},{12,8},{16,20},{20,16},{24,28},{28,24},{1,5},{5... | collective-permute-start | bytes 14254088 | tf_op jit(solution)/shard_map/ppermute | solution.py:94
  205.8 106.1 %collective-permute-start.33 = (bf16[4,2,2,1160,128]{4,3,2,1,0:T(8,128)(2,1)}, bf16[4,2,2,1160,128]{4,3,2,1,0:T(8,128)(2,1)}, u32[]{:S(2)}, u32[]{:S(2)}) collective-permute-start(bf16[4,2,2,1160,128]{4,3,2,1,0:T(8,128)(2,1)} %maximum_maximum_fusion.1), channel_id=1, source_target_pairs={{0,4},{4,0},{8,12},{12,8},{16,20},{20,16},{24,28},{28,24},{1,5},{5... | collective-permute-start | bytes 14254088 | tf_op jit(solution)/shard_map/ppermute | solution.py:94
  248.6 107.5 %collective-permute-start.17 = (bf16[512,2304]{1,0:T(8,128)(2,1)}, bf16[512,2304]{1,0:T(8,128)(2,1)}, u32[]{:S(2)}, u32[]{:S(2)}) collective-permute-start(bf16[512,2304]{1,0:T(8,128)(2,1)} %pad_maximum_fusion.5), channel_id=1, source_target_pairs={{0,1},{1,2},{2,3},{4,5},{5,6},{6,7},{8,9},{9,10},{10,11},{12,13},{... | collective-permute-start | bytes 7077896 | tf_op jit(solution)/shard_map/ppermute | solution.py:381
  253.4 102.6 %collective-permute-start.16 = (bf16[512,2304]{1,0:T(8,128)(2,1)}, bf16[512,2304]{1,0:T(8,128)(2,1)}, u32[]{:S(2)}, u32[]{:S(2)}) collective-permute-start(bf16[512,2304]{1,0:T(8,128)(2,1)} %pad_maximum_fusion.5), channel_id=1, source_target_pairs={{0,2},{1,3},{4,6},{5,7},{8,10},{9,11},{12,14},{13,15},{16,18},{17,... | collective-permute-start | bytes 7077896 | tf_op jit(solution)/shard_map/ppermute | solution.py:381
  478.8 90.9 %collective-permute-start.43 = (bf16[512,1152]{1,0:T(8,128)(2,1)}, bf16[512,1152]{1,0:T(8,128)(2,1)}, u32[]{:S(2)}, u32[]{:S(2)}) collective-permute-start(bf16[512,1152]{1,0:T(8,128)(2,1)} %get-tuple-element.50), channel_id=1, source_target_pairs={{2,0},{3,1},{6,4},{7,5},{10,8},{11,9},{14,12},{15,13},{18,16},{19,... | collective-permute-start | bytes 3538952 | tf_op jit(solution)/shard_map/ppermute | solution.py:427
  480.1 90.1 %collective-permute-start.42 = (bf16[512,1152]{1,0:T(8,128)(2,1)}, bf16[512,1152]{1,0:T(8,128)(2,1)}, u32[]{:S(2)}, u32[]{:S(2)}) collective-permute-start(bf16[512,1152]{1,0:T(8,128)(2,1)} %get-tuple-element.51), channel_id=1, source_target_pairs={{1,0},{2,1},{3,2},{5,4},{6,5},{7,6},{9,8},{10,9},{11,10},{13,12},{... | collective-permute-start | bytes 3538952 | tf_op jit(solution)/shard_map/ppermute | solution.py:427
  483.1 90.3 %collective-permute-start.45 = (bf16[512,1152]{1,0:T(8,128)(2,1)}, bf16[512,1152]{1,0:T(8,128)(2,1)}, u32[]{:S(2)}, u32[]{:S(2)}) collective-permute-start(bf16[512,1152]{1,0:T(8,128)(2,1)} %get-tuple-element.47), channel_id=1, source_target_pairs={{2,0},{3,1},{6,4},{7,5},{10,8},{11,9},{14,12},{15,13},{18,16},{19,... | collective-permute-start | bytes 3538952 | tf_op jit(solution)/shard_map/ppermute | solution.py:427
  484.4 89.0 %collective-permute-start.44 = (bf16[512,1152]{1,0:T(8,128)(2,1)}, bf16[512,1152]{1,0:T(8,128)(2,1)}, u32[]{:S(2)}, u32[]{:S(2)}) collective-permute-start(bf16[512,1152]{1,0:T(8,128)(2,1)} %get-tuple-element.48), channel_id=1, source_target_pairs={{1,0},{2,1},{3,2},{5,4},{6,5},{7,6},{9,8},{10,9},{11,10},{13,12},{... | collective-permute-start | bytes 3538952 | tf_op jit(solution)/shard_map/ppermute | solution.py:427
  496.3 133.7 %collective-permute-start.54 = (bf16[4,2,2,296,128]{4,3,2,1,0:T(8,128)(2,1)}, bf16[4,2,2,296,128]{4,3,2,1,0:T(8,128)(2,1)}, u32[]{:S(2)}, u32[]{:S(2)}) collective-permute-start(bf16[4,2,2,296,128]{4,3,2,1,0:T(8,128)(2,1)} %dynamic-slice_bitcast_fusion.3), channel_id=1, source_target_pairs={{0,4},{4,0},{8,12},{12,8},{16,20},{20,16},{24,28},{28,24},{1,5},{5... | collective-permute-start | bytes 3637256 | tf_op jit(solution)/shard_map/ppermute | solution.py:94
  569.8 199.8 %collective-permute-start.62 = (bf16[4,2,2,1160,128]{4,3,2,1,0:T(8,128)(2,1)}, bf16[4,2,2,1160,128]{4,3,2,1,0:T(8,128)(2,1)}, u32[]{:S(2)}, u32[]{:S(2)}) collective-permute-start(bf16[4,2,2,1160,128]{4,3,2,1,0:T(8,128)(2,1)} %dynamic-slice_bitcast_fusion.1), channel_id=1, source_target_pairs={{0,4},{4,0},{8,12},{12,8},{16,20},{20,16},{24,28},{28,24},{1,5},{5... | collective-permute-start | bytes 14254088 | tf_op jit(solution)/shard_map/ppermute | solution.py:94
  570.3 207.3 %collective-permute-start.70 = (bf16[4,2,2,1160,128]{4,3,2,1,0:T(8,128)(2,1)}, bf16[4,2,2,1160,128]{4,3,2,1,0:T(8,128)(2,1)}, u32[]{:S(2)}, u32[]{:S(2)}) collective-permute-start(bf16[4,2,2,1160,128]{4,3,2,1,0:T(8,128)(2,1)} %dynamic-slice_bitcast_fusion), channel_id=1, source_target_pairs={{0,4},{4,0},{8,12},{12,8},{16,20},{20,16},{24,28},{28,24},{1,5},{5... | collective-permute-start | bytes 14254088 | tf_op jit(solution)/shard_map/ppermute | solution.py:94
  621.5 137.7 %collective-permute-start.46 = (bf16[4,2,2,872,128]{4,3,2,1,0:T(8,128)(2,1)}, bf16[4,2,2,872,128]{4,3,2,1,0:T(8,128)(2,1)}, u32[]{:S(2)}, u32[]{:S(2)}) collective-permute-start(bf16[4,2,2,872,128]{4,3,2,1,0:T(8,128)(2,1)} %dynamic-slice_bitcast_fusion.2), channel_id=1, source_target_pairs={{0,4},{4,0},{8,12},{12,8},{16,20},{20,16},{24,28},{28,24},{1,5},{5... | collective-permute-start | bytes 10715144 | tf_op jit(solution)/shard_map/ppermute | solution.py:94
  631.8 51.1 %collective-permute-start.55 = (bf16[2,2,296,128]{3,2,0,1:T(8,128)(2,1)S(1)}, bf16[2,2,296,128]{3,2,0,1:T(8,128)(2,1)S(1)}, u32[]{:S(2)}, u32[]{:S(2)}) collective-permute-start(bf16[2,2,296,128]{3,2,0,1:T(8,128)(2,1)S(1)} %bitcast.500), channel_id=1, source_target_pairs={{0,1},{1,0},{2,3},{3,2},{4,5},{5,4},{6,7},{7,6},{8,9},{9,8},{10,11... | collective-permute-start | bytes 909320 | tf_op jit(solution)/shard_map/ppermute | solution.py:94
  680.8 37.0 %collective-permute-start.57 = (bf16[2,2,296,128]{3,2,1,0:T(8,128)(2,1)S(1)}, bf16[2,2,296,128]{3,2,1,0:T(8,128)(2,1)S(1)}, u32[]{:S(2)}, u32[]{:S(2)}) collective-permute-start(bf16[2,2,296,128]{3,2,1,0:T(8,128)(2,1)S(1)} %dynamic-slice_bitcast_fusion.13), channel_id=1, source_target_pairs={{0,2},{1,3},{2,0},{3,1},{4,6},{5,7},{6,4},{7,5},{8,10},{9,11},{10,... | collective-permute-start | bytes 909320 | tf_op jit(solution)/shard_map/ppermute | solution.py:94
  682.9 45.5 %collective-permute-start.85 = (f32[8,128]{1,0:T(8,128)S(1)}, f32[8,128]{1,0:T(8,128)S(1)}, u32[]{:S(2)}, u32[]{:S(2)}) collective-permute-start(f32[8,128]{1,0:T(8,128)S(1)} %get-tuple-element.139), channel_id=1, source_target_pairs={{0,24},{4,28},{8,0},{12,4},{16,8},{20,12},{24,16},{28,20},{1,25},{... | collective-permute-start | bytes 12296 | tf_op jit(solution)/shard_map/ppermute | solution.py:94
  776.1 37.3 %collective-permute-start.63 = (bf16[2,2,1160,128]{3,2,0,1:T(8,128)(2,1)}, bf16[2,2,1160,128]{3,2,0,1:T(8,128)(2,1)}, u32[]{:S(2)}, u32[]{:S(2)}) collective-permute-start(bf16[2,2,1160,128]{3,2,0,1:T(8,128)(2,1)} %bitcast.468), channel_id=1, source_target_pairs={{0,1},{1,0},{2,3},{3,2},{4,5},{5,4},{6,7},{7,6},{8,9},{9,8},{10,11... | collective-permute-start | bytes 3563528 | tf_op jit(solution)/shard_map/ppermute | solution.py:94
  777.6 39.2 %collective-permute-start.65 = (bf16[2,2,1160,128]{3,2,1,0:T(8,128)(2,1)}, bf16[2,2,1160,128]{3,2,1,0:T(8,128)(2,1)}, u32[]{:S(2)}, u32[]{:S(2)}) collective-permute-start(bf16[2,2,1160,128]{3,2,1,0:T(8,128)(2,1)} %dynamic-slice_bitcast_fusion.5), channel_id=1, source_target_pairs={{0,2},{1,3},{2,0},{3,1},{4,6},{5,7},{6,4},{7,5},{8,10},{9,11},{10,... | collective-permute-start | bytes 3563528 | tf_op jit(solution)/shard_map/ppermute | solution.py:94
  782.9 55.8 %collective-permute-start.71 = (bf16[2,2,1160,128]{3,2,0,1:T(8,128)(2,1)S(1)}, bf16[2,2,1160,128]{3,2,0,1:T(8,128)(2,1)S(1)}, u32[]{:S(2)}, u32[]{:S(2)}) collective-permute-start(bf16[2,2,1160,128]{3,2,0,1:T(8,128)(2,1)S(1)} %bitcast.495), channel_id=1, source_target_pairs={{0,1},{1,0},{2,3},{3,2},{4,5},{5,4},{6,7},{7,6},{8,9},{9,8},{10,11... | collective-permute-start | bytes 3563528 | tf_op jit(solution)/shard_map/ppermute | solution.py:94
  787.9 53.5 %collective-permute-start.73 = (bf16[2,2,1160,128]{3,2,1,0:T(8,128)(2,1)S(1)}, bf16[2,2,1160,128]{3,2,1,0:T(8,128)(2,1)S(1)}, u32[]{:S(2)}, u32[]{:S(2)}) collective-permute-start(bf16[2,2,1160,128]{3,2,1,0:T(8,128)(2,1)S(1)} %dynamic-slice_bitcast_fusion.4), channel_id=1, source_target_pairs={{0,2},{1,3},{2,0},{3,1},{4,6},{5,7},{6,4},{7,5},{8,10},{9,11},{10,... | collective-permute-start | bytes 3563528 | tf_op jit(solution)/shard_map/ppermute | solution.py:94
  791.5 59.6 %collective-permute-start.48 = (bf16[2,872,128]{2,1,0:T(8,128)(2,1)S(1)}, bf16[2,872,128]{2,1,0:T(8,128)(2,1)S(1)}, u32[]{:S(2)}, u32[]{:S(2)}) collective-permute-start(bf16[2,872,128]{2,1,0:T(8,128)(2,1)S(1)} %dynamic-slice_bitcast_fusion.12), channel_id=1, source_target_pairs={{0,2},{1,3},{2,0},{3,1},{4,6},{5,7},{6,4},{7,5},{8,10},{9,11},{10,... | collective-permute-start | bytes 1339400 | tf_op jit(solution)/shard_map/ppermute | solution.py:94
  813.4 37.8 %collective-permute-start.50 = (bf16[2,872,128]{2,1,0:T(8,128)(2,1)S(1)}, bf16[2,872,128]{2,1,0:T(8,128)(2,1)S(1)}, u32[]{:S(2)}, u32[]{:S(2)}) collective-permute-start(bf16[2,872,128]{2,1,0:T(8,128)(2,1)S(1)} %dynamic-slice_bitcast_fusion.11), channel_id=1, source_target_pairs={{0,1},{1,0},{2,3},{3,2},{4,5},{5,4},{6,7},{7,6},{8,9},{9,8},{10,11... | collective-permute-start | bytes 1339400 | tf_op jit(solution)/shard_map/ppermute | solution.py:94
  816.8 64.2 %collective-permute-start.64 = (bf16[2,1160,128]{2,1,0:T(8,128)(2,1)S(1)}, bf16[2,1160,128]{2,1,0:T(8,128)(2,1)S(1)}, u32[]{:S(2)}, u32[]{:S(2)}) collective-permute-start(bf16[2,1160,128]{2,1,0:T(8,128)(2,1)S(1)} %dynamic-slice_bitcast_fusion.10), channel_id=1, source_target_pairs={{0,2},{1,3},{2,0},{3,1},{4,6},{5,7},{6,4},{7,5},{8,10},{9,11},{10,... | collective-permute-start | bytes 1781768 | tf_op jit(solution)/shard_map/ppermute | solution.py:94
  838.7 42.4 %collective-permute-start.66 = (bf16[2,1160,128]{2,1,0:T(8,128)(2,1)S(1)}, bf16[2,1160,128]{2,1,0:T(8,128)(2,1)S(1)}, u32[]{:S(2)}, u32[]{:S(2)}) collective-permute-start(bf16[2,1160,128]{2,1,0:T(8,128)(2,1)S(1)} %dynamic-slice_bitcast_fusion.9), channel_id=1, source_target_pairs={{0,1},{1,0},{2,3},{3,2},{4,5},{5,4},{6,7},{7,6},{8,9},{9,8},{10,11... | collective-permute-start | bytes 1781768 | tf_op jit(solution)/shard_map/ppermute | solution.py:94
  (153 other events, 2663.3 us)
